TPU v7x, 256 devices: a whole 4x4x8 slice. The times are simulated.
256 devices in a mesh: dp: 16 (over z, core), expert: 16 (over y, x).
Axes of the slice: x: 4, y: 4, z: 8, core: 2. Of those that a mesh axis runs over, the one named last changes fastest.
Arguments:
- tokens: bfloat16 [32768, 1024], P(('dp', 'expert')), may hold values from -6 to 6
- out_grad: bfloat16 [32768, 1024], P(('dp', 'expert')), may hold values from -6 to 6
- route_ids: int32 [32768, 8], P(('dp', 'expert')), may hold values from 0 to 31, all different within a row; in each aligned block of 128 rows (0 to 127, 128 to 255, ...) at most 40 rows name the same one
- route_gates: float32 [32768, 8], P(('dp', 'expert')), may hold values from 0.2 to 1.8
- w_gate: bfloat16 [32, 1024, 512], P('expert', 'dp'), may hold values from -0.1875 to 0.1875
- w_up: bfloat16 [32, 1024, 512], P('expert', 'dp'), may hold values from -0.1875 to 0.1875
- w_down: bfloat16 [32, 512, 1024], P('expert', 'dp'), may hold values from -0.25 to 0.25
Outputs:
- input_grad: bfloat16 [32768, 1024], P(('dp', 'expert'))
- gate_grad: float32 [32768, 8], P(('dp', 'expert'))
- gate_wgrad: float32 [32, 1024, 512], P('expert', 'dp')
- up_wgrad: float32 [32, 1024, 512], P('expert', 'dp')
- down_wgrad: float32 [32, 512, 1024], P('expert', 'dp')
Inputs may be any that keep to these rules, and one draw needn't show every extreme that they name: `route_ids`: each token names 8 different experts. Among the 128 tokens of one device at most 40 name any one expert, and in every draw some device has an expert named by exactly 40 of its tokens.
All inputs are finite; a program needn't handle non-finite values.
Results may differ from a plain program's by a relative error of at most 0.028.
Values may be sent and summed in bfloat16 or wider, within the bound.
No kernel may reach another device: no remote copies, remote signals or barrier semaphores. Data moves between devices by JAX's collectives and lax.ppermute only.
A program may use at most 128 MiB of HBM per device.

v0:
```python
import math

import jax
import jax.numpy as jnp
from jax import lax
from jax.sharding import PartitionSpec as P


def slot_table(route_ids, experts, capacity):
    token_count, top_picks = route_ids.shape
    onehot = (route_ids[:, :, None] == jnp.arange(experts, dtype=jnp.int32)[None, None, :]).astype(
        jnp.int32
    )
    flat_hits = onehot.reshape(token_count * top_picks, experts)
    earlier = jnp.cumsum(flat_hits, axis=0) - flat_hits
    ranked = jnp.sum(earlier * flat_hits, axis=1).reshape(token_count, top_picks)
    return route_ids * capacity + ranked


def expert_rows(rows_in, grads_in, gates_in, w_gate, w_up, w_down):
    contract_rows = (((0,), (0,)), ((), ()))
    contract_last = (((1,), (1,)), ((), ()))
    gate_pre = jnp.dot(rows_in, w_gate, preferred_element_type=jnp.float32)
    up_proj = jnp.dot(rows_in, w_up, preferred_element_type=jnp.float32)
    sigmoid_gate = jax.nn.sigmoid(gate_pre)
    active = gate_pre * sigmoid_gate
    hidden = (active * up_proj).astype(jnp.bfloat16)
    output = jnp.dot(hidden, w_down, preferred_element_type=jnp.float32)
    copy_gate_grad = jnp.sum(output * grads_in.astype(jnp.float32), axis=1)
    scaled = (gates_in[:, None] * grads_in.astype(jnp.float32)).astype(jnp.bfloat16)
    hidden_grad = lax.dot_general(scaled, w_down, contract_last, preferred_element_type=jnp.float32)
    up_grad = (hidden_grad * active).astype(jnp.bfloat16)
    pre_grad = (
        hidden_grad * up_proj * (sigmoid_gate * (1.0 + gate_pre * (1.0 - sigmoid_gate)))
    ).astype(jnp.bfloat16)
    copy_input_grad = (
        lax.dot_general(pre_grad, w_gate, contract_last, preferred_element_type=jnp.float32)
        + lax.dot_general(up_grad, w_up, contract_last, preferred_element_type=jnp.float32)
    ).astype(jnp.bfloat16)
    gate_part = lax.dot_general(
        rows_in, pre_grad, contract_rows, preferred_element_type=jnp.float32
    )
    up_part = lax.dot_general(rows_in, up_grad, contract_rows, preferred_element_type=jnp.float32)
    down_part = lax.dot_general(hidden, scaled, contract_rows, preferred_element_type=jnp.float32)
    return (copy_input_grad, copy_gate_grad, gate_part, up_part, down_part)


def shards(tokens, out_grad, route_ids, route_gates, w_gate, w_up, w_down):
    contract_rows = (((0,), (0,)), ((), ()))
    dp_size = lax.axis_size("dp")
    expert_size = lax.axis_size("expert")
    local_experts = w_gate.shape[0]
    experts = local_experts * expert_size
    token_count, top_picks = route_ids.shape
    model_width = tokens.shape[1]
    capacity = 5 * token_count * top_picks // (4 * experts)
    slot_count = experts * capacity
    scale = 1.0 / math.sqrt(token_count * dp_size * top_picks / local_experts)
    slot_ids = slot_table(route_ids, experts, capacity)
    onehot = (
        slot_ids[:, :, None] == jnp.arange(slot_count, dtype=jnp.int32)[None, None, :]
    ).astype(jnp.float32)
    dispatch = jnp.sum(onehot, axis=1).astype(jnp.bfloat16)
    send_rows = lax.dot_general(dispatch, tokens, contract_rows, preferred_element_type=jnp.float32)
    send_rows = send_rows.astype(jnp.bfloat16).reshape(experts, capacity, model_width)
    send_grads = lax.dot_general(
        dispatch, out_grad, contract_rows, preferred_element_type=jnp.float32
    )
    send_grads = send_grads.astype(jnp.bfloat16).reshape(experts, capacity, model_width)
    send_gates = jnp.einsum(
        "tks,tk->s", onehot, route_gates, precision=lax.Precision.HIGHEST
    ).reshape(experts, capacity)
    whole_gate, whole_up, whole_down = (
        lax.all_gather(w_gate, "dp", axis=1, tiled=True),
        lax.all_gather(w_up, "dp", axis=1, tiled=True),
        lax.all_gather(w_down, "dp", axis=1, tiled=True),
    )
    rows_in, grads_in, gates_in = (
        lax.all_to_all(send_rows, "expert", split_axis=0, concat_axis=1, tiled=True),
        lax.all_to_all(send_grads, "expert", split_axis=0, concat_axis=1, tiled=True),
        lax.all_to_all(
            send_gates.astype(jnp.bfloat16), "expert", split_axis=0, concat_axis=1, tiled=True
        ).astype(send_gates.dtype),
    )
    results = []
    for member in range(local_experts):
        parts = expert_rows(
            rows_in[member],
            grads_in[member],
            gates_in[member],
            whole_gate[member],
            whole_up[member],
            whole_down[member],
        )
        results.append(parts)
    input_rows = jnp.stack([entry[0] for entry in results])
    gate_rows = jnp.stack([entry[1] for entry in results])
    gate_sum, up_sum, down_sum = (
        lax.psum_scatter(
            jnp.stack([entry[2] for entry in results]).astype(jnp.bfloat16),
            "dp",
            scatter_dimension=1,
            tiled=True,
        ).astype(jnp.float32),
        lax.psum_scatter(
            jnp.stack([entry[3] for entry in results]).astype(jnp.bfloat16),
            "dp",
            scatter_dimension=1,
            tiled=True,
        ).astype(jnp.float32),
        lax.psum_scatter(
            jnp.stack([entry[4] for entry in results]).astype(jnp.bfloat16),
            "dp",
            scatter_dimension=1,
            tiled=True,
        ).astype(jnp.float32),
    )
    back_rows, back_gates = (
        lax.all_to_all(input_rows, "expert", split_axis=1, concat_axis=0, tiled=True),
        lax.all_to_all(
            gate_rows.astype(jnp.bfloat16), "expert", split_axis=1, concat_axis=0, tiled=True
        ).astype(gate_rows.dtype),
    )
    input_grad = jnp.dot(
        dispatch, back_rows.reshape(slot_count, model_width), preferred_element_type=jnp.float32
    )
    gate_grad = jnp.einsum(
        "tks,s->tk", onehot, back_gates.reshape(slot_count), precision=lax.Precision.HIGHEST
    )
    return (
        input_grad.astype(jnp.bfloat16),
        gate_grad,
        gate_sum * scale,
        up_sum * scale,
        down_sum * scale,
    )


def solution(mesh):
    return jax.shard_map(
        shards,
        mesh=mesh,
        in_specs=(
            P(("dp", "expert"), None),
            P(("dp", "expert"), None),
            P(("dp", "expert"), None),
            P(("dp", "expert"), None),
            P("expert", "dp", None),
            P("expert", "dp", None),
            P("expert", "dp", None),
        ),
        out_specs=(
            P(("dp", "expert"), None),
            P(("dp", "expert"), None),
            P("expert", "dp", None),
            P("expert", "dp", None),
            P("expert", "dp", None),
        ),
        check_vma=False,
    )
```

profile of v0, /device:TPU:1, one launch (start us, length us, event | category | flops | bytes accessed | tf_op | source)
XLA Modules:
  0.0 334.3 jit_solution(3824946793698170015)
XLA Ops:
  10.5 9.0 %reduce-window.6 = s32[32,8,128]{2,1,0:T(8,128)S(1)} reduce-window(s32[32,8,128]{2,1,0:T(8,128)S(1)} %fusion.32, s32[]{:T(128)} %constant.6.clone.1), window={size=1x1x128 pad=0_0x0_0x127_0}, to_apply=%region_0.0 | reduce-window | flops 4161536 | bytes 262148 | tf_op jit(solution)/shard_map/reduce-window
  22.6 7.6 %all-to-all-start = ((bf16[16,2,40]{2,1,0:T(2,128)(2,1)}), bf16[16,2,40]{2,1,0:T(2,128)(2,1)S(1)}, u32[]{:S(2)}, u32[]{:S(2)}) async-start(bf16[16,2,40]{2,1,0:T(2,128)(2,1)} %convert_element_type.117), calls=%async_computation | async-start | bytes 16384 | tf_op jit(solution)/shard_map/all_to_all | solution.py:81
  31.8 2.4 convolution_convert_fusion.1
  34.2 2.3 all-to-all-done
  36.5 4.5 %all-to-all-start.1 = ((bf16[32,40,1024]{2,1,0:T(8,128)(2,1)}), bf16[32,40,1024]{2,1,0:T(8,128)(2,1)S(1)}, u32[]{:S(2)}, u32[]{:S(2)}) async-start(bf16[32,40,1024]{2,1,0:T(8,128)(2,1)} %bitcast.137), calls=%async_computation.1 | async-start | bytes 5242880 | tf_op jit(solution)/shard_map/all_to_all | solution.py:80
  41.7 2.4 convolution_convert_fusion
  44.1 33.6 %all-to-all-done.1 = bf16[32,40,1024]{2,1,0:T(8,128)(2,1)S(1)} async-done(((bf16[32,40,1024]{2,1,0:T(8,128)(2,1)}), bf16[32,40,1024]{2,1,0:T(8,128)(2,1)S(1)}, u32[]{:S(2)}, u32[]{:S(2)}) %all-to-all-start.1) | async-done | bytes 2621472 | tf_op jit(solution)/shard_map/all_to_all | solution.py:80
  79.3 4.6 %all-to-all-start.2 = ((bf16[32,40,1024]{2,1,0:T(8,128)(2,1)}), bf16[32,40,1024]{2,1,0:T(8,128)(2,1)}, u32[]{:S(2)}, u32[]{:S(2)}) async-start(bf16[32,40,1024]{2,1,0:T(8,128)(2,1)} %bitcast.136), calls=%async_computation.2 | async-start | bytes 5242880 | tf_op jit(solution)/shard_map/all_to_all | solution.py:79
  86.3 31.1 %all-to-all-done.2 = bf16[32,40,1024]{2,1,0:T(8,128)(2,1)} async-done(((bf16[32,40,1024]{2,1,0:T(8,128)(2,1)}), bf16[32,40,1024]{2,1,0:T(8,128)(2,1)}, u32[]{:S(2)}, u32[]{:S(2)}) %all-to-all-start.2) | async-done | bytes 2621472 | tf_op jit(solution)/shard_map/all_to_all | solution.py:79
  117.4 3.5 %fusion.37 = (bf16[1,16,40,1024]{3,2,0,1:T(8,128)(2,1)}, bf16[1,16,40,1024]{3,2,0,1:T(8,128)(2,1)}) fusion(bf16[2,16,40,1024]{3,2,0,1:T(8,128)(2,1)} %bitcast.12), kind=kLoop, calls=%fused_computation.87 | loop fusion | bytes 5242880 | tf_op jit(solution)/shard_map/slice | solution.py:88
  123.0 3.5 %fusion.28 = f32[640,512]{1,0:T(8,128)} fusion(bf16[640,1024]{1,0:T(8,128)(2,1)} %bitcast.144, bf16[2,1024,512]{2,1,0:T(8,128)(2,1)} %all-gather.8.cloned.1.call-done), kind=kOutput, calls=%fused_computation.66 | convolution fusion | flops 671088640 | bytes 3670016 | tf_op jit(solution)/shard_map/dot_general | solution.py:23
  126.5 3.6 %fusion.25 = f32[640,512]{1,0:T(8,128)} fusion(bf16[640,1024]{1,0:T(8,128)(2,1)} %bitcast.149, bf16[2,512,1024]{2,1,0:T(8,128)(2,1)} %all-gather.4.cloned.1.call-done), kind=kOutput, calls=%fused_computation.63 | convolution fusion | flops 671088640 | bytes 3670016 | tf_op jit(solution)/shard_map/dot_general | solution.py:31
  130.1 3.8 %all-gather.6.cloned.1.call-done = bf16[2,1024,512]{2,1,0:T(8,128)(2,1)} async-done(((bf16[2,64,512]{2,1,0:T(8,128)(2,1)}), bf16[2,1024,512]{2,1,0:T(8,128)(2,1)}) %all-gather.6.cloned.1.call-update) | async-done | bytes 2097168 | tf_op jit(solution)/shard_map/all_gather | solution.py:75
  133.9 4.9 %multiply_convert_fusion = (bf16[640,512]{1,0:T(8,128)(2,1)}, bf16[640,512]{1,0:T(8,128)(2,1)}, bf16[640,512]{1,0:T(8,128)(2,1)S(1)}) fusion(f32[640,512]{1,0:T(8,128)} %fusion.28, f32[640,512]{1,0:T(8,128)} %fusion.25, bf16[640,1024]{1,0:T(8,128)(2,1)} %bitcast.145, bf16[2,1024,512]{2,1,0:T(8,128)(2,1)} %all-gather.6.cloned.1.call-done), kind=kOutput, calls=%fused_computation.41 | convolution fusion | flops 676003840 | bytes 6946816 | tf_op jit(solution)/shard_map/dot_general | solution.py:24
  144.6 2.4 multiply_convert_fusion.1
  149.6 2.6 fusion.13
  160.2 2.5 fusion.6
  163.4 6.5 %all-to-all-start.4 = ((bf16[2,16,40]{2,0,1:T(2,128)(2,1)}), bf16[2,16,40]{2,0,1:T(2,128)(2,1)S(1)}, u32[]{:S(2)}, u32[]{:S(2)}) async-start(bf16[2,16,40]{2,0,1:T(2,128)(2,1)} %copy.72), calls=%async_computation.4 | async-start | bytes 16384 | tf_op jit(solution)/shard_map/all_to_all | solution.py:120
  181.7 4.2 %copy.69 = bf16[2,640,1024]{2,0,1:T(2,128)(2,1)} copy(bf16[2,640,1024]{2,1,0:T(8,128)(2,1)S(1)} %pad_maximum_fusion) | data formatting | bytes 5242880 | tf_op jit(solution)/shard_map/stack | solution.py:96
  185.9 6.7 %all-to-all-start.3 = ((bf16[2,640,1024]{2,0,1:T(2,128)(2,1)}), bf16[2,640,1024]{2,0,1:T(2,128)(2,1)S(1)}, u32[]{:S(2)}, u32[]{:S(2)}) async-start(bf16[2,640,1024]{2,0,1:T(2,128)(2,1)} %copy.69), calls=%async_computation.3 | async-start | bytes 5242880 | tf_op jit(solution)/shard_map/all_to_all | solution.py:119
  192.7 5.9 %fusion = f32[1,128,8]{2,0,1:T(1,128)S(1)} fusion(bf16[1280,1,1]{0,1,2:T(2,128)(2,1)S(1)} %reshape.108, s32[128,8]{1,0:T(8,128)S(1)} %copy.67), kind=kOutput, calls=%fused_computation.2 | convolution fusion | flops 3932160 | bytes 10752 | tf_op jit(solution)/shard_map/tks,s->tk/dot_general | solution.py:127
  199.3 31.6 %all-to-all-done.3 = bf16[2,640,1024]{2,0,1:T(2,128)(2,1)S(1)} async-done(((bf16[2,640,1024]{2,0,1:T(2,128)(2,1)}), bf16[2,640,1024]{2,0,1:T(2,128)(2,1)S(1)}, u32[]{:S(2)}, u32[]{:S(2)}) %all-to-all-start.3) | async-done | bytes 2621472 | tf_op jit(solution)/shard_map/all_to_all | solution.py:119
  234.8 31.3 %reduce-scatter.4.cloned.1.call-done = bf16[2,64,512]{2,1,0:T(8,128)(2,1)} async-done(((bf16[2,1024,512]{2,1,0:T(8,128)(2,1)}), bf16[2,64,512]{2,1,0:T(8,128)(2,1)}) %reduce-scatter.4.cloned.1.call-update) | async-done | bytes 131088 | tf_op jit(solution)/shard_map/reduce_scatter | solution.py:99
  267.8 58.0 %reduce-scatter.8.cloned.1.call-done = bf16[2,32,1024]{2,1,0:T(8,128)(2,1)} async-done(((bf16[2,512,1024]{2,1,0:T(8,128)(2,1)}), bf16[2,32,1024]{2,1,0:T(8,128)(2,1)}) %reduce-scatter.8.cloned.1.call-update) | async-done | bytes 131088 | tf_op jit(solution)/shard_map/reduce_scatter | solution.py:111
  (125 shorter events, 51.2 us)
Async XLA Ops:
  7.2 24.6 %copy-start = (bf16[128,1024]{1,0:T(8,128)(2,1)S(1)}, bf16[128,1024]{1,0:T(8,128)(2,1)}, u32[]{:S(2)}) copy-start(bf16[128,1024]{1,0:T(8,128)(2,1)} %param.8) | copy-start | bytes 786436
  7.2 12.9 %copy-start.22 = (s32[128,8]{0,1:T(8,128)S(1)}, s32[128,8]{0,1:T(8,128)}, u32[]{:S(2)}) copy-start(s32[128,8]{0,1:T(8,128)} %param.9) | copy-start | bytes 12292
  7.2 115.8 %all-gather.8.cloned.1.call-start = ((), (), s32[]{:S(2)}) async-start(), calls=%async_computation.10 | async-start | bytes 2228224 | tf_op jit(solution)/shard_map/all_gather | solution.py:74
  7.9 118.6 %all-gather.4.cloned.1.call-start = ((), (), s32[]{:S(2)}) async-start(), calls=%async_computation.8 | async-start | bytes 2228224 | tf_op jit(solution)/shard_map/all_gather | solution.py:76
  22.6 13.9 %all-to-all-start = ((bf16[16,2,40]{2,1,0:T(2,128)(2,1)}), bf16[16,2,40]{2,1,0:T(2,128)(2,1)S(1)}, u32[]{:S(2)}, u32[]{:S(2)}) async-start(bf16[16,2,40]{2,1,0:T(2,128)(2,1)} %convert_element_type.117), calls=%async_computation | async-start | bytes 16384 | tf_op jit(solution)/shard_map/all_to_all | solution.py:81
  36.5 5.2 %copy-start.21 = (bf16[128,1024]{1,0:T(8,128)(2,1)S(1)}, bf16[128,1024]{1,0:T(8,128)(2,1)}, u32[]{:S(2)}) copy-start(bf16[128,1024]{1,0:T(8,128)(2,1)} %param.7) | copy-start | bytes 786436
  36.5 41.2 %all-to-all-start.1 = ((bf16[32,40,1024]{2,1,0:T(8,128)(2,1)}), bf16[32,40,1024]{2,1,0:T(8,128)(2,1)S(1)}, u32[]{:S(2)}, u32[]{:S(2)}) async-start(bf16[32,40,1024]{2,1,0:T(8,128)(2,1)} %bitcast.137), calls=%async_computation.1 | async-start | bytes 5242880 | tf_op jit(solution)/shard_map/all_to_all | solution.py:80
  41.0 92.9 %all-gather.6.cloned.1.call-start = ((), (), s32[]{:S(2)}) async-start(), calls=%async_computation.9 | async-start | bytes 2228224 | tf_op jit(solution)/shard_map/all_gather | solution.py:75
  79.3 38.1 %all-to-all-start.2 = ((bf16[32,40,1024]{2,1,0:T(8,128)(2,1)}), bf16[32,40,1024]{2,1,0:T(8,128)(2,1)}, u32[]{:S(2)}, u32[]{:S(2)}) async-start(bf16[32,40,1024]{2,1,0:T(8,128)(2,1)} %bitcast.136), calls=%async_computation.2 | async-start | bytes 5242880 | tf_op jit(solution)/shard_map/all_to_all | solution.py:79
  83.9 149.3 %reduce-scatter.6.cloned.1.call-start = ((), (), s32[]{:S(2)}) async-start(), calls=%async_computation.12 | async-start | bytes 2228224 | tf_op jit(solution)/shard_map/reduce_scatter | solution.py:105
  133.9 4.9 %copy-start.9 = (bf16[1,16,40,1024]{3,2,0,1:T(8,128)(2,1)S(1)}, bf16[1,16,40,1024]{3,2,0,1:T(8,128)(2,1)}, u32[]{:S(2)}) copy-start(bf16[1,16,40,1024]{3,2,0,1:T(8,128)(2,1)} %get-tuple-element.20) | copy-start | bytes 3932164
  138.8 2.2 copy-start.7
  149.6 116.6 %reduce-scatter.4.cloned.1.call-start = ((), (), s32[]{:S(2)}) async-start(), calls=%async_computation.11 | async-start | bytes 2228224 | tf_op jit(solution)/shard_map/reduce_scatter | solution.py:99
  149.6 2.7 copy-start.8
  149.6 2.7 copy-start.19
  156.4 2.0 copy-start.24
  156.4 2.5 copy-start.25
  160.2 10.0 %copy-start.11 = (bf16[640,1024]{1,0:T(8,128)(2,1)S(1)}, bf16[640,1024]{1,0:T(8,128)(2,1)}, u32[]{:S(2)}) copy-start(bf16[640,1024]{1,0:T(8,128)(2,1)} %get-tuple-element.7) | copy-start | bytes 3932164
  163.4 22.5 %all-to-all-start.4 = ((bf16[2,16,40]{2,0,1:T(2,128)(2,1)}), bf16[2,16,40]{2,0,1:T(2,128)(2,1)S(1)}, u32[]{:S(2)}, u32[]{:S(2)}) async-start(bf16[2,16,40]{2,0,1:T(2,128)(2,1)} %copy.72), calls=%async_computation.4 | async-start | bytes 16384 | tf_op jit(solution)/shard_map/all_to_all | solution.py:120
  170.0 155.9 %reduce-scatter.8.cloned.1.call-start = ((), (), s32[]{:S(2)}) async-start(), calls=%async_computation.13 | async-start | bytes 2228224 | tf_op jit(solution)/shard_map/reduce_scatter | solution.py:111
  170.2 2.2 copy-start.10
  170.2 2.2 copy-start.26
  185.9 44.9 %all-to-all-start.3 = ((bf16[2,640,1024]{2,0,1:T(2,128)(2,1)}), bf16[2,640,1024]{2,0,1:T(2,128)(2,1)S(1)}, u32[]{:S(2)}, u32[]{:S(2)}) async-start(bf16[2,640,1024]{2,0,1:T(2,128)(2,1)} %copy.69), calls=%async_computation.3 | async-start | bytes 5242880 | tf_op jit(solution)/shard_map/all_to_all | solution.py:119
  232.0 95.5 %copy-start.1 = (bf16[128,1024]{1,0:T(8,128)(2,1)S(1)}, bf16[128,1024]{1,0:T(8,128)(2,1)}, u32[]{:S(2)}) copy-start(bf16[128,1024]{1,0:T(8,128)(2,1)} %param.8) | copy-start | bytes 786436
  (14 other events, 20.4 us)
Sparse Core Ops, SparseCore 0:
  9.9 43.7 all-gather.7
  55.6 38.0 all-gather.3
  95.5 38.2 all-gather.5
  149.7 55.4 reduce-scatter.5
  207.5 58.5 reduce-scatter.3
  268.6 57.2 reduce-scatter.7
where the time goes:
time: 338 us; the launch traced here: 334 us
  waiting for transfers between devices  194 us (57%)
  matrix products  45.4 us (13%)
  starting transfers between devices  30.5 us (9%)
  local copies, waits for them, and re-layouts  25.3 us (7%)
  other arithmetic  24.6 us (7%)
  between operations  14.6 us (4%)
    reduce_scatter x1, waiting for transfers between devices, shards(): lax.psum_scatter(jnp.stack([entry[4] for entry in results]).astype(jnp.bf...  58 us
    all_to_all x1, waiting for transfers between devices, shards(): lax.all_to_all(send_grads, 'expert', split_axis=0, concat_axis=1, tiled=T...  33.6 us
    all_to_all x1, waiting for transfers between devices, shards(): lax.all_to_all(input_rows, 'expert', split_axis=1, concat_axis=0, tiled=T...  31.6 us
    reduce_scatter x1, waiting for transfers between devices, shards(): lax.psum_scatter(jnp.stack([entry[2] for entry in results]).astype(jnp.bf...  31.3 us
    all_to_all x1, waiting for transfers between devices, shards(): lax.all_to_all(send_rows, 'expert', split_axis=0, concat_axis=1, tiled=True)  31.1 us
    unnamed x56, local copies, waits for them, and re-layouts  9.85 us
    another operation x3, other arithmetic  9.15 us
    all_to_all x1, starting transfers between devices, shards(): lax.all_to_all(send_gates.astype(jnp.bfloat16), 'expert', split_axis=0, c...  7.58 us
  transfers between devices with their start and end apart: 11, of which 7 were waited for; matrix products, arithmetic and copies ran while one was open for 22% of the time, Pallas kernels for 0%

commit v1 on v0

v1 whole, which is shorter than its diff:
```python
import math

import jax
import jax.numpy as jnp
from jax import lax
from jax.experimental import pallas as pl
from jax.experimental.pallas import tpu as pltpu
from jax.sharding import PartitionSpec as P

F32 = jnp.float32
BF16 = jnp.bfloat16
LANES = 128
VMEM_LIMIT = 56 * 1024 * 1024


def dot(a, b, ca, cb):
    return lax.dot_general(a, b, (((ca,), (cb,)), ((), ())), preferred_element_type=F32)


def split_high_low(x):
    high = x.astype(BF16)
    return high, (x - high.astype(F32)).astype(BF16)


def named_by_expert(ids, values, experts):
    top, tokens = ids.shape
    row = lax.broadcasted_iota(jnp.int32, (experts, tokens), 0)
    total = jnp.zeros((experts, tokens), F32)
    for k in range(top):
        total = total + jnp.where(ids[k : k + 1, :] == row, values[k : k + 1, :], 0.0)
    return total


def dispatch_kernel(ids_ref, gates_ref, tokens_ref, grads_ref, send_ref, slots_ref):
    experts, capacity, _ = send_ref.shape
    token_count, width = tokens_ref.shape
    ids = ids_ref[...]
    named = named_by_expert(ids, jnp.ones(ids.shape, F32), experts)
    gates = named_by_expert(ids, gates_ref[...], experts)
    earlier = lax.broadcasted_iota(jnp.int32, (token_count, token_count), 0)
    later = lax.broadcasted_iota(jnp.int32, (token_count, token_count), 1)
    before = jnp.where(earlier < later, 1.0, 0.0).astype(BF16)
    ranks = dot(named.astype(BF16), before, 1, 0)
    key = jnp.where(named > 0.0, ranks, -1.0)
    shape = (experts, capacity, token_count)
    place = lax.broadcasted_iota(jnp.int32, shape, 1).astype(F32)
    hit = key[:, None, :] == place
    slots = jnp.where(hit, 1.0, 0.0).reshape(experts * capacity, token_count).astype(BF16)
    slots_ref[...] = slots
    weighted = jnp.where(hit, gates[:, None, :], 0.0).reshape(experts * capacity, token_count)
    high, low = split_high_low(weighted)
    rows = dot(slots, tokens_ref[...], 1, 0)
    send_ref[:, :, :width] = rows.astype(BF16).reshape(experts, capacity, width)
    grads = grads_ref[...]
    both = jnp.concatenate([high, low], axis=1)
    scaled = dot(both, jnp.concatenate([grads, grads], axis=0), 1, 0)
    send_ref[:, :, width:] = scaled.astype(BF16).reshape(experts, capacity, width)


def expert_kernel(recv_ref, weights_ref, parts_ref, pre_ref, up_ref, gate_ref):
    sources, _, capacity, _ = recv_ref.shape
    pieces, _, depth, hidden_width = weights_ref.shape
    share = depth // 3
    half = share // 2
    rows_count = sources * capacity
    width = pieces * share

    def weight(start, size):
        return weights_ref[:, 0, start : start + size, :].reshape(pieces * size, hidden_width)

    w_gate = weight(0, share)
    w_up = weight(share, share)
    down_left = weight(2 * share, half)
    down_right = weight(2 * share + half, half)
    rows = recv_ref[:, 0, :, :width].reshape(rows_count, width)
    scaled = recv_ref[:, 0, :, width:].reshape(rows_count, width)
    cut = width // 2
    gate_pre = dot(rows, w_gate, 1, 0)
    up_proj = dot(rows, w_up, 1, 0)
    hidden_grad = dot(scaled[:, :cut], down_left, 1, 1) + dot(scaled[:, cut:], down_right, 1, 1)
    sig = jax.nn.sigmoid(gate_pre)
    act = gate_pre * sig
    hidden = (act * up_proj).astype(BF16)
    up_grad = (hidden_grad * act).astype(BF16)
    pre_grad = (hidden_grad * up_proj * (sig * (1.0 + gate_pre * (1.0 - sig)))).astype(BF16)
    pre_ref[0] = pre_grad
    up_ref[0] = up_grad
    gate_grad = jnp.sum(hidden.astype(F32) * hidden_grad, axis=1, keepdims=True)
    high, low = split_high_low(jnp.broadcast_to(gate_grad, (rows_count, LANES)))
    lane = lax.broadcasted_iota(jnp.int32, (rows_count, LANES), 1)
    gate_ref[0] = jnp.where(lane < LANES // 2, high.astype(F32), low.astype(F32)).astype(BF16)

    def put(start, size, value):
        parts_ref[:, 0, start : start + size, :] = value.astype(BF16).reshape(
            pieces, size, hidden_width
        )

    put(0, share, dot(rows, pre_grad, 0, 0))
    put(share, share, dot(rows, up_grad, 0, 0))
    put(2 * share, half, dot(hidden, scaled[:, :cut], 0, 0))
    put(2 * share + half, half, dot(hidden, scaled[:, cut:], 0, 0))


def input_kernel(pre_ref, up_ref, gate_ref, weights_ref, back_ref):
    sources, _, capacity, total_width = back_ref.shape
    pieces, _, depth, hidden_width = weights_ref.shape
    share = depth // 2
    width = pieces * share
    w_gate = weights_ref[:, 0, :share, :].reshape(width, hidden_width)
    w_up = weights_ref[:, 0, share:, :].reshape(width, hidden_width)
    grad = dot(pre_ref[0], w_gate, 1, 1) + dot(up_ref[0], w_up, 1, 1)
    back_ref[:, 0, :, :width] = grad.astype(BF16).reshape(sources, capacity, width)
    back_ref[:, 0, :, width:] = gate_ref[0].reshape(sources, capacity, total_width - width)


def combine_kernel(ids_ref, gates_ref, slots_ref, back_ref, input_ref, gate_ref):
    experts, capacity, _ = back_ref.shape
    top, token_count = ids_ref.shape
    width = input_ref.shape[1]
    slot_count = experts * capacity
    slots = slots_ref[...]
    rows = back_ref[:, :, :width].reshape(slot_count, width)
    input_ref[...] = dot(slots, rows, 0, 0).astype(BF16)
    extra = back_ref[:, :, width:].astype(F32)
    value = (extra[:, :, :1] + extra[:, :, LANES // 2 : LANES // 2 + 1]).reshape(slot_count, 1)
    picked = jnp.where(slots.astype(F32) > 0.0, value, 0.0)
    by_expert = jnp.sum(picked.reshape(experts, capacity, token_count), axis=1)
    row = lax.broadcasted_iota(jnp.int32, (experts, token_count), 0)
    ids = ids_ref[...]
    for k in range(top):
        own = jnp.where(ids[k : k + 1, :] == row, by_expert, 0.0)
        gate_ref[k : k + 1, :] = jnp.sum(own, axis=0, keepdims=True) / gates_ref[k : k + 1, :]


def shards(tokens, out_grad, route_ids, route_gates, w_gate, w_up, w_down):
    dp_size = lax.axis_size("dp")
    expert_size = lax.axis_size("expert")
    members, share, hidden_width = w_gate.shape
    half = share // 2
    experts = members * expert_size
    token_count, top = route_ids.shape
    width = tokens.shape[1]
    capacity = 5 * token_count * top // (4 * experts)
    slot_count = experts * capacity
    rows_count = expert_size * capacity
    scale = 1.0 / math.sqrt(token_count * dp_size * top / members)
    params = pltpu.CompilerParams(vmem_limit_bytes=VMEM_LIMIT)

    packed = jnp.concatenate(
        [w_gate, w_up, w_down[:, :, :hidden_width], w_down[:, :, hidden_width:]], axis=1
    )
    weights = lax.all_gather(packed, "dp", axis=0, tiled=False)

    ids = route_ids.T
    gates = route_gates.T
    send, slots = pl.pallas_call(
        dispatch_kernel,
        out_shape=(
            jax.ShapeDtypeStruct((experts, capacity, 2 * width), BF16),
            jax.ShapeDtypeStruct((slot_count, token_count), BF16),
        ),
        compiler_params=params,
        name="dispatch",
    )(ids, gates, tokens, out_grad)
    recv = lax.all_to_all(send, "expert", split_axis=0, concat_axis=0, tiled=True)
    recv = recv.reshape(expert_size, members, capacity, 2 * width)

    whole = lambda *shape: pl.BlockSpec(shape, lambda m: (0, m, 0, 0))
    own = lambda *shape: pl.BlockSpec(shape, lambda m: (m, 0, 0))
    depth = 3 * share
    parts, pre_grad, up_grad, gate_rows = pl.pallas_call(
        expert_kernel,
        grid=(members,),
        in_specs=[
            whole(expert_size, 1, capacity, 2 * width),
            whole(dp_size, 1, depth, hidden_width),
        ],
        out_specs=(
            whole(dp_size, 1, depth, hidden_width),
            own(1, rows_count, hidden_width),
            own(1, rows_count, hidden_width),
            own(1, rows_count, LANES),
        ),
        out_shape=(
            jax.ShapeDtypeStruct((dp_size, members, depth, hidden_width), BF16),
            jax.ShapeDtypeStruct((members, rows_count, hidden_width), BF16),
            jax.ShapeDtypeStruct((members, rows_count, hidden_width), BF16),
            jax.ShapeDtypeStruct((members, rows_count, LANES), BF16),
        ),
        compiler_params=params,
        name="expert",
    )(recv, weights)
    sums = lax.psum_scatter(parts, "dp", scatter_dimension=0, tiled=False)

    back = pl.pallas_call(
        input_kernel,
        grid=(members,),
        in_specs=[
            own(1, rows_count, hidden_width),
            own(1, rows_count, hidden_width),
            own(1, rows_count, LANES),
            whole(dp_size, 1, 2 * share, hidden_width),
        ],
        out_specs=whole(expert_size, 1, capacity, width + LANES),
        out_shape=jax.ShapeDtypeStruct((expert_size, members, capacity, width + LANES), BF16),
        compiler_params=params,
        name="inputs",
    )(pre_grad, up_grad, gate_rows, weights)
    back = lax.all_to_all(
        back.reshape(experts, capacity, width + LANES),
        "expert",
        split_axis=0,
        concat_axis=0,
        tiled=True,
    )
    input_grad, gate_grad = pl.pallas_call(
        combine_kernel,
        out_shape=(
            jax.ShapeDtypeStruct((token_count, width), BF16),
            jax.ShapeDtypeStruct((top, token_count), F32),
        ),
        compiler_params=params,
        name="combine",
    )(ids, gates, slots, back)

    sums = sums.astype(F32) * scale
    down = jnp.concatenate(
        [sums[:, 2 * share : 2 * share + half], sums[:, 2 * share + half :]], axis=2
    )
    return (input_grad, gate_grad.T, sums[:, :share], sums[:, share : 2 * share], down)


def solution(mesh):
    return jax.shard_map(
        shards,
        mesh=mesh,
        in_specs=(
            P(("dp", "expert"), None),
            P(("dp", "expert"), None),
            P(("dp", "expert"), None),
            P(("dp", "expert"), None),
            P("expert", "dp", None),
            P("expert", "dp", None),
            P("expert", "dp", None),
        ),
        out_specs=(
            P(("dp", "expert"), None),
            P(("dp", "expert"), None),
            P("expert", "dp", None),
            P("expert", "dp", None),
            P("expert", "dp", None),
        ),
        check_vma=False,
    )
```

time: 338 us -> 177 us (0.52)
  waiting for transfers between devices: 194 us -> 15.4 us
  blocking collectives: 0 us -> 109 us
  matrix products: 45.4 us -> 0 us
  starting transfers between devices: 30.5 us -> 0.08 us
  Pallas kernels: 0 us -> 29.7 us
  local copies, waits for them, and re-layouts: 25.3 us -> 1.73 us
  other arithmetic: 24.6 us -> 3.54 us
    all_to_all x0 -> x2, blocking collectives: none -> 109 us  [the longest x1 68.8 us: shards(): lax.all_to_all(send, 'expert', split_axis=0, concat_axis=0, tiled=True)]
    all_to_all x5 -> x0, waiting for transfers between devices: 98.6 us -> none  [the longest x1 33.6 us: shards(): lax.all_to_all(send_grads, 'expert', split_axis=0, concat_axis=1, tiled=T...]
    reduce_scatter x3 -> x1, waiting for transfers between devices: 89.4 us -> 15.4 us  [shards(): sums = lax.psum_scatter(parts, 'dp', scatter_dimension=0, tiled=False)]
    dot_general x23 -> x0, matrix products: 45.4 us -> none  [the longest x2 7.29 us: expert_rows(): up_proj = jnp.dot(rows_in, w_up, preferred_element_type=jnp.float32)]
    all_to_all x5 -> x0, starting transfers between devices: 29.9 us -> none  [the longest x1 7.58 us: shards(): lax.all_to_all(send_gates.astype(jnp.bfloat16), 'expert', split_axis=0, c...]
    pallas_call x0 -> x4, Pallas kernels: none -> 29.7 us  [the longest x1 14.9 us: shards(): pl.pallas_call(expert_kernel, grid=(members,), in_specs=[whole(expert_siz...]
    another operation x8 -> x0, other arithmetic: 14 us -> none
    unnamed x56 -> x0, local copies, waits for them, and re-layouts: 9.85 us -> none
  transfers between devices with their start and end apart: 11 -> 2, of which waited for: 7 -> 1; matrix products, arithmetic and copies ran while one was open for 22% -> 0% of each run, Pallas kernels for 0% -> 9%
where the time goes in v1:
time: 177 us; the launch traced here: 174 us
  blocking collectives  109 us (62%)
  Pallas kernels  29.7 us (17%)
  waiting for transfers between devices  15.4 us (9%)
  between operations  14.1 us (8%)
  other arithmetic  3.54 us (2%)
    all_to_all x1, blocking collectives, shards(): lax.all_to_all(send, 'expert', split_axis=0, concat_axis=0, tiled=True)  68.8 us
    all_to_all x1, blocking collectives, shards(): lax.all_to_all(back.reshape(experts, capacity, width + LANES), 'expert',...  40.3 us
    reduce_scatter x1, waiting for transfers between devices, shards(): sums = lax.psum_scatter(parts, 'dp', scatter_dimension=0, tiled=False)  15.4 us
    pallas_call x1, Pallas kernels, shards(): pl.pallas_call(expert_kernel, grid=(members,), in_specs=[whole(expert_siz...  14.9 us
    pallas_call x1, Pallas kernels, shards(): pl.pallas_call(input_kernel, grid=(members,), in_specs=[own(1, rows_count...  6.42 us
    pallas_call x1, Pallas kernels, shards(): pl.pallas_call(dispatch_kernel, out_shape=(jax.ShapeDtypeStruct((experts,...  5.12 us
  transfers between devices with their start and end apart: 2, of which 1 were waited for; matrix products, arithmetic and copies ran while one was open for 0% of the time, Pallas kernels for 9%

profile of v1, /device:TPU:1, one launch (start us, length us, event | category | flops | bytes accessed | tf_op | source)
XLA Modules:
  0.0 173.6 jit_solution(8791461458541171833)
XLA Ops:
  7.2 0.0 all-gather.3.cloned.1.call-start
  7.2 0.9 fusion.2
  8.1 1.7 %pad_maximum_fusion = bf16[2,192,512]{2,1,0:T(8,128)(2,1)} fusion(bf16[2,32,512]{2,1,0:T(8,128)(2,1)S(1)} %get-tuple-element.26, bf16[2,32,512]{2,1,0:T(8,128)(2,1)S(1)} %get-tuple-element.25, bf16[2,64,512]{2,1,0:T(8,128)(2,1)} %param.12, bf16[2,64,512]{2,1,0:T(8,128)(2,1)} %param.11), kind=kLoop, calls=%fused_computation.1 | loop fusion | flops 1572864 | bytes 786432 | tf_op jit(solution)/shard_map/concatenate | solution.py:149
  9.8 0.0 all-gather.3.cloned.1.call-update
  9.9 0.0 reduce-scatter.2.cloned.1.call-start
  9.9 5.1 %dispatch.1 = (bf16[32,40,2048]{2,1,0:T(8,128)(2,1)}, bf16[1280,128]{1,0:T(8,128)(2,1)}) custom-call(s32[8,128]{1,0:T(8,128)} %bitcast.12, f32[8,128]{1,0:T(8,128)} %bitcast.14, bf16[128,1024]{1,0:T(8,128)(2,1)} %tokens_ref.1, bf16[128,1024]{1,0:T(8,128)(2,1)} %grads_ref.1), custom_call_target="tpu_custom_call" | custom-call | tf_op jit(solution)/shard_map/dispatch/pallas_call | solution.py:156
  15.0 68.8 %all_to_all.10 = bf16[32,40,2048]{2,1,0:T(8,128)(2,1)} all-to-all(bf16[32,40,2048]{2,1,0:T(8,128)(2,1)} %get-tuple-element.14), channel_id=1, replica_groups=mesh['dp'=16,'expert'=16] {'expert'}, dimensions={0} | all-to-all | bytes 10485760 | tf_op jit(solution)/shard_map/all_to_all | solution.py:165
  83.8 0.0 all-gather.3.cloned.1.call-done
  83.8 14.9 %expert.1 = (bf16[16,2,192,512]{3,2,1,0:T(8,128)(2,1)}, bf16[2,640,512]{2,1,0:T(8,128)(2,1)}, bf16[2,640,512]{2,1,0:T(8,128)(2,1)}, bf16[2,640,128]{2,1,0:T(8,128)(2,1)}) custom-call(bf16[16,2,40,2048]{3,2,1,0:T(8,128)(2,1)} %bitcast.10, bf16[16,2,192,512]{3,2,1,0:T(8,128)(2,1)} %bitcast.8), custom_call_target="tpu_custom_call" | custom-call | tf_op jit(solution)/shard_map/expert/pallas_call | solution.py:171
  98.7 0.0 reduce-scatter.2.cloned.1.call-update
  98.7 6.4 %inputs.1 = bf16[16,2,40,1152]{3,2,1,0:T(8,128)(2,1)} custom-call(bf16[2,640,512]{2,1,0:T(8,128)(2,1)} %get-tuple-element.15.pre_ref, bf16[2,640,512]{2,1,0:T(8,128)(2,1)} %get-tuple-element.16.up_ref, bf16[2,640,128]{2,1,0:T(8,128)(2,1)} %get-tuple-element.17.gate_ref, bf16[16,2,192,512]{3,2,1,0:T(8,128)(2,1)} %bitcast.9), custom_call_target="tpu_custom_call" | custom-call | tf_op jit(solution)/shard_map/inputs/pallas_call | solution.py:195
  105.1 40.3 %all_to_all.11.back_ref = bf16[32,40,1152]{2,1,0:T(8,128)(2,1)} all-to-all(bf16[32,40,1152]{2,1,0:T(8,128)(2,1)} %bitcast.11), channel_id=1, replica_groups=mesh['dp'=16,'expert'=16] {'expert'}, dimensions={0} | all-to-all | bytes 5898240 | tf_op jit(solution)/shard_map/all_to_all | solution.py:209
  145.4 3.3 %combine.1 = (bf16[128,1024]{1,0:T(8,128)(2,1)}, f32[8,128]{1,0:T(8,128)}) custom-call(s32[8,128]{1,0:T(8,128)} %bitcast.13, f32[8,128]{1,0:T(8,128)} %bitcast.15, bf16[1280,128]{1,0:T(8,128)(2,1)} %get-tuple-element.13.slots_ref, bf16[32,40,1152]{2,1,0:T(8,128)(2,1)} %all_to_all.11.back_ref), custom_call_target="tpu_custom_call" | custom-call | tf_op jit(solution)/shard_map/combine/pallas_call | solution.py:216
  148.7 15.4 %reduce-scatter.2.cloned.1.call-done = bf16[1,2,192,512]{3,2,1,0:T(8,128)(2,1)} async-done(((bf16[16,2,192,512]{3,2,1,0:T(8,128)(2,1)}), bf16[1,2,192,512]{3,2,1,0:T(8,128)(2,1)}) %reduce-scatter.2.cloned.1.call-update) | async-done | bytes 393232 | tf_op jit(solution)/shard_map/reduce_scatter | solution.py:193
  164.1 1.1 multiply_bitcast_fusion
  165.2 0.8 fusion.1
  166.0 0.7 pad_maximum_fusion.1
  (1 shorter events, 0.0 us)
Async XLA Ops:
  7.2 76.6 %all-gather.3.cloned.1.call-start = ((), (), s32[]{:S(2)}) async-start(), calls=%async_computation.4 | async-start | bytes 6684672 | tf_op jit(solution)/shard_map/all_gather | solution.py:152
  9.9 154.2 %reduce-scatter.2.cloned.1.call-start = ((), (), s32[]{:S(2)}) async-start(), calls=%async_computation.3 | async-start | bytes 6684672 | tf_op jit(solution)/shard_map/reduce_scatter | solution.py:193
Sparse Core Ops, SparseCore 0:
  10.0 50.2 all-gather.2
  98.8 65.2 reduce-scatter.1

commit v2 on v1

--- a/solution.py
+++ b/solution.py
@@ -1,3 +1,4 @@
+import functools
 import math
 
 import jax
@@ -31,7 +32,29 @@
     return total
 
 
-def dispatch_kernel(ids_ref, gates_ref, tokens_ref, grads_ref, send_ref, slots_ref):
+def pack_weights(gate_ref, up_ref, down_ref, packed_ref):
+    share = gate_ref.shape[1]
+    half = share // 2
+    hidden_width = gate_ref.shape[2]
+    packed_ref[:, :share] = gate_ref[...]
+    packed_ref[:, share : 2 * share] = up_ref[...]
+    packed_ref[:, 2 * share : 2 * share + half] = down_ref[:, :, :hidden_width]
+    packed_ref[:, 2 * share + half :] = down_ref[:, :, hidden_width:]
+
+
+def dispatch_kernel(
+    ids_ref,
+    gates_ref,
+    tokens_ref,
+    grads_ref,
+    w_gate_ref,
+    w_up_ref,
+    w_down_ref,
+    send_ref,
+    slots_ref,
+    packed_ref,
+):
+    pack_weights(w_gate_ref, w_up_ref, w_down_ref, packed_ref)
     experts, capacity, _ = send_ref.shape
     token_count, width = tokens_ref.shape
     ids = ids_ref[...]
@@ -57,7 +80,9 @@
     send_ref[:, :, width:] = scaled.astype(BF16).reshape(experts, capacity, width)
 
 
-def expert_kernel(recv_ref, weights_ref, parts_ref, pre_ref, up_ref, gate_ref):
+def expert_kernel(
+    core_ref, recv_ref, weights_ref, keep_ref, give_ref, pre_ref, up_ref, gate_ref
+):
     sources, _, capacity, _ = recv_ref.shape
     pieces, _, depth, hidden_width = weights_ref.shape
     share = depth // 3
@@ -90,10 +115,20 @@
     lane = lax.broadcasted_iota(jnp.int32, (rows_count, LANES), 1)
     gate_ref[0] = jnp.where(lane < LANES // 2, high.astype(F32), low.astype(F32)).astype(BF16)
 
+    core = core_ref[0]
+
     def put(start, size, value):
-        parts_ref[:, 0, start : start + size, :] = value.astype(BF16).reshape(
-            pieces, size, hidden_width
-        )
+        value = value.astype(BF16).reshape(pieces // 2, 2, size, hidden_width)
+
+        @pl.when(core == 0)
+        def _():
+            keep_ref[:, 0, start : start + size, :] = value[:, 0]
+            give_ref[:, 0, start : start + size, :] = value[:, 1]
+
+        @pl.when(core == 1)
+        def _():
+            keep_ref[:, 0, start : start + size, :] = value[:, 1]
+            give_ref[:, 0, start : start + size, :] = value[:, 0]
 
     put(0, share, dot(rows, pre_grad, 0, 0))
     put(share, share, dot(rows, up_grad, 0, 0))
@@ -132,6 +167,20 @@
         gate_ref[k : k + 1, :] = jnp.sum(own, axis=0, keepdims=True) / gates_ref[k : k + 1, :]
 
 
+def scale_kernel(scale, sums_ref, gate_ref, up_ref, down_ref):
+    share = gate_ref.shape[1]
+    half = share // 2
+    hidden_width = gate_ref.shape[2]
+
+    def part(start, size):
+        return sums_ref[:, start : start + size].astype(F32) * scale
+
+    gate_ref[...] = part(0, share)
+    up_ref[...] = part(share, share)
+    down_ref[:, :, :hidden_width] = part(2 * share, half)
+    down_ref[:, :, hidden_width:] = part(2 * share + half, half)
+
+
 def shards(tokens, out_grad, route_ids, route_gates, w_gate, w_up, w_down):
     dp_size = lax.axis_size("dp")
     expert_size = lax.axis_size("expert")
@@ -146,51 +195,52 @@
     scale = 1.0 / math.sqrt(token_count * dp_size * top / members)
     params = pltpu.CompilerParams(vmem_limit_bytes=VMEM_LIMIT)
 
-    packed = jnp.concatenate(
-        [w_gate, w_up, w_down[:, :, :hidden_width], w_down[:, :, hidden_width:]], axis=1
-    )
-    weights = lax.all_gather(packed, "dp", axis=0, tiled=False)
-
     ids = route_ids.T
     gates = route_gates.T
-    send, slots = pl.pallas_call(
+    depth = 3 * share
+    send, slots, packed = pl.pallas_call(
         dispatch_kernel,
         out_shape=(
             jax.ShapeDtypeStruct((experts, capacity, 2 * width), BF16),
             jax.ShapeDtypeStruct((slot_count, token_count), BF16),
+            jax.ShapeDtypeStruct((members, depth, hidden_width), BF16),
         ),
         compiler_params=params,
         name="dispatch",
-    )(ids, gates, tokens, out_grad)
+    )(ids, gates, tokens, out_grad, w_gate, w_up, w_down)
+    weights = lax.all_gather(packed, "dp", axis=0, tiled=False)
     recv = lax.all_to_all(send, "expert", split_axis=0, concat_axis=0, tiled=True)
     recv = recv.reshape(expert_size, members, capacity, 2 * width)
 
     whole = lambda *shape: pl.BlockSpec(shape, lambda m: (0, m, 0, 0))
     own = lambda *shape: pl.BlockSpec(shape, lambda m: (m, 0, 0))
-    depth = 3 * share
-    parts, pre_grad, up_grad, gate_rows = pl.pallas_call(
+    core = lax.rem(lax.axis_index("dp"), 2).astype(jnp.int32).reshape(1)
+    keep, give, pre_grad, up_grad, gate_rows = pl.pallas_call(
         expert_kernel,
         grid=(members,),
         in_specs=[
+            pl.BlockSpec(memory_space=pltpu.SMEM),
             whole(expert_size, 1, capacity, 2 * width),
             whole(dp_size, 1, depth, hidden_width),
         ],
         out_specs=(
-            whole(dp_size, 1, depth, hidden_width),
+            whole(dp_size // 2, 1, depth, hidden_width),
+            whole(dp_size // 2, 1, depth, hidden_width),
             own(1, rows_count, hidden_width),
             own(1, rows_count, hidden_width),
             own(1, rows_count, LANES),
         ),
         out_shape=(
-            jax.ShapeDtypeStruct((dp_size, members, depth, hidden_width), BF16),
+            jax.ShapeDtypeStruct((dp_size // 2, members, depth, hidden_width), BF16),
+            jax.ShapeDtypeStruct((dp_size // 2, members, depth, hidden_width), BF16),
             jax.ShapeDtypeStruct((members, rows_count, hidden_width), BF16),
             jax.ShapeDtypeStruct((members, rows_count, hidden_width), BF16),
             jax.ShapeDtypeStruct((members, rows_count, LANES), BF16),
         ),
         compiler_params=params,
         name="expert",
-    )(recv, weights)
-    sums = lax.psum_scatter(parts, "dp", scatter_dimension=0, tiled=False)
+    )(core, recv, weights)
+    got = lax.ppermute(give, "dp", [(i, i ^ 1) for i in range(dp_size)])
 
     back = pl.pallas_call(
         input_kernel,
@@ -206,6 +256,11 @@
         compiler_params=params,
         name="inputs",
     )(pre_grad, up_grad, gate_rows, weights)
+    pair_sum = keep + got
+    same_core = [list(range(c, dp_size, 2)) for c in range(2)]
+    sums = lax.psum_scatter(
+        pair_sum, "dp", scatter_dimension=0, tiled=False, axis_index_groups=same_core
+    )
     back = lax.all_to_all(
         back.reshape(experts, capacity, width + LANES),
         "expert",
@@ -223,11 +278,13 @@
         name="combine",
     )(ids, gates, slots, back)
 
-    sums = sums.astype(F32) * scale
-    down = jnp.concatenate(
-        [sums[:, 2 * share : 2 * share + half], sums[:, 2 * share + half :]], axis=2
-    )
-    return (input_grad, gate_grad.T, sums[:, :share], sums[:, share : 2 * share], down)
+    gate_sum, up_sum, down_sum = pl.pallas_call(
+        functools.partial(scale_kernel, scale),
+        out_shape=tuple(jax.ShapeDtypeStruct(w.shape, F32) for w in (w_gate, w_up, w_down)),
+        compiler_params=params,
+        name="scale",
+    )(sums)
+    return (input_grad, gate_grad.T, gate_sum, up_sum, down_sum)
 
 
 def solution(mesh):

time: 177 us -> 187 us (1.056); the launches traced: 174 us -> 187 us
  waiting for transfers between devices: 15.4 us -> 82.8 us
  blocking collectives: 109 us -> 42.1 us
  starting transfers between devices: 0.08 us -> 9.54 us
  Pallas kernels: 29.7 us -> 33.3 us
    all_to_all x0 -> x1, waiting for transfers between devices: none -> 77.3 us  [shards(): lax.all_to_all(send, 'expert', split_axis=0, concat_axis=0, tiled=True)]
    all_to_all x1 -> x0, blocking collectives: 68.8 us -> none  [shards(): lax.all_to_all(send, 'expert', split_axis=0, concat_axis=0, tiled=True)]
    reduce_scatter x1, waiting for transfers between devices: 15.4 us -> 0.01 us  [shards(): lax.psum_scatter(pair_sum, 'dp', scatter_dimension=0, tiled=False, axis_i...]
    all_to_all x0 -> x1, starting transfers between devices: none -> 7.66 us  [shards(): lax.all_to_all(send, 'expert', split_axis=0, concat_axis=0, tiled=True)]
    ppermute x0 -> x1, waiting for transfers between devices: none -> 5.5 us  [shards(): got = lax.ppermute(give, 'dp', [(i, i ^ 1) for i in range(dp_size)])]
    add x0 -> x1, other arithmetic: none -> 4.65 us  [shards(): pair_sum = keep + got]
    pallas_call x1 -> x2, Pallas kernels: 14.9 us -> 18.5 us  [the longest x1 16.5 us: shards(): pl.pallas_call(expert_kernel, grid=(members,), in_specs=[pl.BlockSpec(mem...]
    concatenate x2 -> x0, other arithmetic: 2.46 us -> none  [the longest x1 1.74 us: shards(): jnp.concatenate([w_gate, w_up, w_down[:, :, :hidden_width], w_down[:, :,...]
  transfers between devices with their start and end apart: 2 -> 4, of which waited for: 1 -> 2; matrix products, arithmetic and copies ran while one was open for 0% -> 0% of each run, Pallas kernels for 9% -> 5%
where the time goes in v2:
time: 187 us
  waiting for transfers between devices  82.8 us (44%)
  blocking collectives  42.1 us (23%)
  Pallas kernels  33.3 us (18%)
  between operations  14.1 us (8%)
  starting transfers between devices  9.54 us (5%)
  other arithmetic  4.65 us (2%)
    all_to_all x1, waiting for transfers between devices, shards(): lax.all_to_all(send, 'expert', split_axis=0, concat_axis=0, tiled=True)  77.3 us
    all_to_all x1, blocking collectives, shards(): lax.all_to_all(back.reshape(experts, capacity, width + LANES), 'expert',...  42.1 us
    pallas_call x1, Pallas kernels, shards(): pl.pallas_call(expert_kernel, grid=(members,), in_specs=[pl.BlockSpec(mem...  16.5 us
    all_to_all x1, starting transfers between devices, shards(): lax.all_to_all(send, 'expert', split_axis=0, concat_axis=0, tiled=True)  7.66 us
    pallas_call x1, Pallas kernels, shards(): pl.pallas_call(input_kernel, grid=(members,), in_specs=[own(1, rows_count...  6.4 us
    ppermute x1, waiting for transfers between devices, shards(): got = lax.ppermute(give, 'dp', [(i, i ^ 1) for i in range(dp_size)])  5.5 us
    pallas_call x1, Pallas kernels, shards(): pl.pallas_call(dispatch_kernel, out_shape=(jax.ShapeDtypeStruct((experts,...  5.23 us
    add x1, other arithmetic, shards(): pair_sum = keep + got  4.65 us
  transfers between devices with their start and end apart: 4, of which 2 were waited for; matrix products, arithmetic and copies ran while one was open for 0% of the time, Pallas kernels for 5%

profile of v2, /device:TPU:1, one launch (start us, length us, event | category | flops | bytes accessed | tf_op | source)
XLA Modules:
  0.0 186.6 jit_solution(3775148160354108133)
XLA Ops:
  7.2 0.0 all-gather.3.cloned.1.call-start
  7.2 5.2 %dispatch.1 = (bf16[32,40,2048]{2,1,0:T(8,128)(2,1)}, bf16[1280,128]{1,0:T(8,128)(2,1)}, bf16[2,192,512]{2,1,0:T(8,128)(2,1)}) custom-call(s32[8,128]{1,0:T(8,128)} %bitcast.12, f32[8,128]{1,0:T(8,128)} %bitcast.14, bf16[128,1024]{1,0:T(8,128)(2,1)} %tokens_ref.1, bf16[128,1024]{1,0:T(8,128)(2,1)} %grads_ref.1, bf16[2,64,512]{2,1,0:T(8,128)(2,1)} %w_gate_ref.1, ...), custom_call_target="tpu_custom_call" | custom-call | tf_op jit(solution)/shard_map/dispatch/pallas_call | solution.py:201
  12.4 0.0 all-gather.3.cloned.1.call-update
  12.5 7.7 %all-to-all-start = ((bf16[32,40,2048]{2,1,0:T(8,128)(2,1)}), bf16[32,40,2048]{2,1,0:T(8,128)(2,1)}, u32[]{:S(2)}, u32[]{:S(2)}) async-start(bf16[32,40,2048]{2,1,0:T(8,128)(2,1)} %get-tuple-element.19), calls=%async_computation | async-start | bytes 10485760 | tf_op jit(solution)/shard_map/all_to_all | solution.py:212
  20.1 0.0 reduce-scatter.2.cloned.1.call-start
  20.2 77.3 %all-to-all-done = bf16[32,40,2048]{2,1,0:T(8,128)(2,1)} async-done(((bf16[32,40,2048]{2,1,0:T(8,128)(2,1)}), bf16[32,40,2048]{2,1,0:T(8,128)(2,1)}, u32[]{:S(2)}, u32[]{:S(2)}) %all-to-all-start) | async-done | bytes 5242912 | tf_op jit(solution)/shard_map/all_to_all | solution.py:212
  97.5 0.0 all-gather.3.cloned.1.call-done
  97.5 16.5 %expert.1 = (bf16[8,2,192,512]{3,2,1,0:T(8,128)(2,1)}, bf16[8,2,192,512]{3,2,1,0:T(8,128)(2,1)}, bf16[2,640,512]{2,1,0:T(8,128)(2,1)}, bf16[2,640,512]{2,1,0:T(8,128)(2,1)}, bf16[2,640,128]{2,1,0:T(8,128)(2,1)}) custom-call(s32[1]{0:T(128)} %bitcast.2.core_ref, bf16[16,2,40,2048]{3,2,1,0:T(8,128)(2,1)} %bitcast.3.recv_ref, bf16[16,2,192,512]{3,2,1,0:T(8,128)(2,1)} %bitcast.8), custom_call_target="tpu_custom_call" | custom-call | tf_op jit(solution)/shard_map/expert/pallas_call | solution.py:218
  114.0 1.8 collective-permute-start
  115.8 5.5 %collective-permute-done = bf16[8,2,192,512]{3,2,1,0:T(8,128)(2,1)S(1)} collective-permute-done((bf16[8,2,192,512]{3,2,1,0:T(8,128)(2,1)}, bf16[8,2,192,512]{3,2,1,0:T(8,128)(2,1)S(1)}, u32[]{:S(2)}, u32[]{:S(2)}) %collective-permute-start) | collective-permute-done | bytes 3145760 | tf_op jit(solution)/shard_map/ppermute | solution.py:243
  121.3 4.6 %add.5 = bf16[8,2,192,512]{3,2,1,0:T(8,128)(2,1)} add(bf16[8,2,192,512]{3,2,1,0:T(8,128)(2,1)} %get-tuple-element.26, bf16[8,2,192,512]{3,2,1,0:T(8,128)(2,1)S(1)} %collective-permute-done) | non-fusion elementwise | flops 1572864 | bytes 9437184 | tf_op jit(solution)/shard_map/add | solution.py:259
  126.0 0.0 reduce-scatter.2.cloned.1.call-update
  126.0 6.4 %inputs.1 = bf16[16,2,40,1152]{3,2,1,0:T(8,128)(2,1)} custom-call(bf16[2,640,512]{2,1,0:T(8,128)(2,1)} %get-tuple-element.21.pre_ref, bf16[2,640,512]{2,1,0:T(8,128)(2,1)} %get-tuple-element.22.up_ref, bf16[2,640,128]{2,1,0:T(8,128)(2,1)} %get-tuple-element.23.gate_ref, bf16[16,2,192,512]{3,2,1,0:T(8,128)(2,1)} %bitcast.9), custom_call_target="tpu_custom_call" | custom-call | tf_op jit(solution)/shard_map/inputs/pallas_call | solution.py:245
  132.4 42.1 %all_to_all.10.back_ref = bf16[32,40,1152]{2,1,0:T(8,128)(2,1)} all-to-all(bf16[32,40,1152]{2,1,0:T(8,128)(2,1)} %bitcast.10), channel_id=1, replica_groups=mesh['dp'=16,'expert'=16] {'expert'}, dimensions={0} | all-to-all | bytes 5898240 | tf_op jit(solution)/shard_map/all_to_all | solution.py:264
  174.6 3.2 %combine.1 = (bf16[128,1024]{1,0:T(8,128)(2,1)}, f32[8,128]{1,0:T(8,128)}) custom-call(s32[8,128]{1,0:T(8,128)} %bitcast.13, f32[8,128]{1,0:T(8,128)} %bitcast.15, bf16[1280,128]{1,0:T(8,128)(2,1)} %get-tuple-element.18.slots_ref, bf16[32,40,1152]{2,1,0:T(8,128)(2,1)} %all_to_all.10.back_ref), custom_call_target="tpu_custom_call" | custom-call | tf_op jit(solution)/shard_map/combine/pallas_call | solution.py:271
  177.8 0.0 reduce-scatter.2.cloned.1.call-done
  177.8 1.9 %scale.1 = (f32[2,64,512]{2,1,0:T(8,128)}, f32[2,64,512]{2,1,0:T(8,128)}, f32[2,32,1024]{2,1,0:T(8,128)}) custom-call(bf16[2,192,512]{2,1,0:T(8,128)(2,1)} %bitcast.11), custom_call_target="tpu_custom_call" | custom-call | tf_op jit(solution)/shard_map/scale/pallas_call | solution.py:281
Async XLA Ops:
  7.2 90.3 %all-gather.3.cloned.1.call-start = ((), (), s32[]{:S(2)}) async-start(), calls=%async_computation.4 | async-start | bytes 6684672 | tf_op jit(solution)/shard_map/all_gather | solution.py:211
  12.5 85.0 %all-to-all-start = ((bf16[32,40,2048]{2,1,0:T(8,128)(2,1)}), bf16[32,40,2048]{2,1,0:T(8,128)(2,1)}, u32[]{:S(2)}, u32[]{:S(2)}) async-start(bf16[32,40,2048]{2,1,0:T(8,128)(2,1)} %get-tuple-element.19), calls=%async_computation | async-start | bytes 10485760 | tf_op jit(solution)/shard_map/all_to_all | solution.py:212
  20.1 157.7 %reduce-scatter.2.cloned.1.call-start = ((), (), s32[]{:S(2)}) async-start(), calls=%async_computation.3 | async-start | bytes 3538944 | tf_op jit(solution)/shard_map/reduce_scatter | solution.py:261
  114.0 7.3 %collective-permute-start = (bf16[8,2,192,512]{3,2,1,0:T(8,128)(2,1)}, bf16[8,2,192,512]{3,2,1,0:T(8,128)(2,1)S(1)}, u32[]{:S(2)}, u32[]{:S(2)}) collective-permute-start(bf16[8,2,192,512]{3,2,1,0:T(8,128)(2,1)} %get-tuple-element.27), channel_id=1, source_target_pairs={{0,16},{16,0},{32,48},{48,32},{64,80},{80,64},{96,112},{112,96},{1... | collective-permute-start | bytes 9437192 | tf_op jit(solution)/shard_map/ppermute | solution.py:243
Sparse Core Ops, SparseCore 0:
  12.6 50.2 all-gather.2
  126.1 45.0 reduce-scatter.1

commit v3 on v2

v3 whole, which is shorter than its diff:
```python
import functools
import math

import jax
import jax.numpy as jnp
from jax import lax
from jax.experimental import pallas as pl
from jax.experimental.pallas import tpu as pltpu
from jax.sharding import PartitionSpec as P

F32 = jnp.float32
BF16 = jnp.bfloat16
LANES = 128
VMEM_LIMIT = 56 * 1024 * 1024
DISPATCH_STEPS = 4
EXPERT_STEPS = 4
INPUT_STEPS = 4


def dot(a, b, ca, cb):
    return lax.dot_general(a, b, (((ca,), (cb,)), ((), ())), preferred_element_type=F32)


def split_high_low(x):
    high = x.astype(BF16)
    return high, (x - high.astype(F32)).astype(BF16)


def expert_of_row(shape, members):
    row = lax.broadcasted_iota(jnp.int32, shape, 0)
    per_member = shape[0] // members
    return lax.rem(row, per_member) * members + row // per_member


def pack_weights(gate_ref, up_ref, down_ref, packed_ref):
    share = gate_ref.shape[1]
    half = share // 2
    hidden_width = gate_ref.shape[2]
    packed_ref[:, :share] = gate_ref[...]
    packed_ref[:, share : 2 * share] = up_ref[...]
    packed_ref[:, 2 * share : 2 * share + half] = down_ref[:, :, :hidden_width]
    packed_ref[:, 2 * share + half :] = down_ref[:, :, hidden_width:]


def dispatch_kernel(
    members,
    experts,
    ids_ref,
    gates_ref,
    tokens_ref,
    grads_ref,
    w_gate_ref,
    w_up_ref,
    w_down_ref,
    send_ref,
    slots_ref,
    packed_ref,
    key_ref,
    gate_ref,
):
    block, capacity, _ = send_ref.shape
    token_count, width = tokens_ref.shape
    step = pl.program_id(0)

    @pl.when(step == 0)
    def _():
        pack_weights(w_gate_ref, w_up_ref, w_down_ref, packed_ref)
        ids = ids_ref[...]
        expert = expert_of_row((experts, token_count), members)
        named = jnp.zeros((experts, token_count), F32)
        gates = jnp.zeros((experts, token_count), F32)
        for k in range(ids.shape[0]):
            same = ids[k : k + 1, :] == expert
            named = named + jnp.where(same, 1.0, 0.0)
            gates = gates + jnp.where(same, gates_ref[k : k + 1, :], 0.0)
        earlier = lax.broadcasted_iota(jnp.int32, (token_count, token_count), 0)
        later = lax.broadcasted_iota(jnp.int32, (token_count, token_count), 1)
        before = jnp.where(earlier < later, 1.0, 0.0).astype(BF16)
        ranks = dot(named.astype(BF16), before, 1, 0)
        key_ref[...] = jnp.where(named > 0.0, ranks, -1.0)
        gate_ref[...] = gates

    start = pl.multiple_of(step * block, block)
    key = key_ref[pl.ds(start, block), :]
    gates = gate_ref[pl.ds(start, block), :]
    place = lax.broadcasted_iota(jnp.int32, (block, capacity, token_count), 1).astype(F32)
    hit = key[:, None, :] == place
    slots = jnp.where(hit, 1.0, 0.0).reshape(block * capacity, token_count).astype(BF16)
    slots_ref[...] = slots
    weighted = jnp.where(hit, gates[:, None, :], 0.0).reshape(block * capacity, token_count)
    high, low = split_high_low(weighted)
    rows = dot(slots, tokens_ref[...], 1, 0)
    send_ref[:, :, :width] = rows.astype(BF16).reshape(block, capacity, width)
    grads = grads_ref[...]
    both = jnp.concatenate([high, low], axis=1)
    scaled = dot(both, jnp.concatenate([grads, grads], axis=0), 1, 0)
    send_ref[:, :, width:] = scaled.astype(BF16).reshape(block, capacity, width)


def expert_kernel(
    steps,
    core_ref,
    recv_ref,
    weights_ref,
    parts_ref,
    grads_ref,
    gate_ref,
    rows_all,
    scaled_all,
    grads_all,
    hidden_all,
):
    sources, capacity, _ = recv_ref.shape
    pieces, _, depth, hidden_width = weights_ref.shape
    share = depth // 3
    half = share // 2
    count = sources * capacity
    width = pieces * share
    step = pl.program_id(0)

    def weight(start, size):
        return weights_ref[:, 0, start : start + size, :].reshape(pieces * size, hidden_width)

    @pl.when(step < steps)
    def _():
        where = pl.ds(pl.multiple_of(step * count, count), count)
        rows = recv_ref[:, :, :width].reshape(count, width)
        scaled = recv_ref[:, :, width:].reshape(count, width)
        rows_all[where, :] = rows
        scaled_all[where, :] = scaled
        down = jnp.concatenate([weight(2 * share, half), weight(2 * share + half, half)], axis=1)
        gate_pre = dot(rows, weight(0, share), 1, 0)
        up_proj = dot(rows, weight(share, share), 1, 0)
        hidden_grad = dot(scaled, down, 1, 1)
        sig = jax.nn.sigmoid(gate_pre)
        act = gate_pre * sig
        hidden = (act * up_proj).astype(BF16)
        up_grad = (hidden_grad * act).astype(BF16)
        pre_grad = (hidden_grad * up_proj * (sig * (1.0 + gate_pre * (1.0 - sig)))).astype(BF16)
        grads = jnp.concatenate([pre_grad, up_grad], axis=1)
        grads_ref[...] = grads
        grads_all[where, :] = grads
        hidden_all[where, :] = hidden
        gate_grad = jnp.sum(hidden.astype(F32) * hidden_grad, axis=1, keepdims=True)
        high, low = split_high_low(jnp.broadcast_to(gate_grad, (count, LANES)))
        lane = lax.broadcasted_iota(jnp.int32, (count, LANES), 1)
        gate_ref[...] = jnp.where(lane < LANES // 2, high.astype(F32), low.astype(F32)).astype(BF16)

    for k in range(2):

        @pl.when(step == steps + k)
        def _(k=k):
            own = grads_all[:, k * hidden_width : (k + 1) * hidden_width]
            total = dot(rows_all[...], own, 0, 0).astype(BF16)
            parts_ref[...] = total.reshape(pieces, share, hidden_width)

    @pl.when(step == steps + 2)
    def _():
        total = dot(hidden_all[...], scaled_all[...], 0, 0).astype(BF16)
        parts_ref[:, :half, :] = total[:, :hidden_width].reshape(pieces, half, hidden_width)
        parts_ref[:, half:, :] = total[:, hidden_width:].reshape(pieces, half, hidden_width)


def input_kernel(core_ref, grads_ref, gate_ref, weights_ref, back_ref):
    sources, capacity, total_width = back_ref.shape
    pieces, _, depth, hidden_width = weights_ref.shape
    share = depth // 2
    width = pieces * share
    w_gate = weights_ref[:, 0, :share, :].reshape(width, hidden_width)
    w_up = weights_ref[:, 0, share:, :].reshape(width, hidden_width)
    grad = dot(grads_ref[...], jnp.concatenate([w_gate, w_up], axis=1), 1, 1)
    back_ref[:, :, :width] = grad.astype(BF16).reshape(sources, capacity, width)
    back_ref[:, :, width:] = gate_ref[...].reshape(sources, capacity, total_width - width)


def combine_kernel(members, ids_ref, gates_ref, slots_ref, back_ref, input_ref, gate_ref):
    experts, capacity, _ = back_ref.shape
    top, token_count = ids_ref.shape
    width = input_ref.shape[1]
    slot_count = experts * capacity
    slots = slots_ref[...]
    rows = back_ref[:, :, :width].reshape(slot_count, width)
    input_ref[...] = dot(slots, rows, 0, 0).astype(BF16)
    extra = back_ref[:, :, width:].astype(F32)
    value = (extra[:, :, :1] + extra[:, :, LANES // 2 : LANES // 2 + 1]).reshape(slot_count, 1)
    picked = jnp.where(slots.astype(F32) > 0.0, value, 0.0)
    by_expert = jnp.sum(picked.reshape(experts, capacity, token_count), axis=1)
    expert = expert_of_row((experts, token_count), members)
    ids = ids_ref[...]
    for k in range(top):
        own = jnp.where(ids[k : k + 1, :] == expert, by_expert, 0.0)
        gate_ref[k : k + 1, :] = jnp.sum(own, axis=0, keepdims=True) / gates_ref[k : k + 1, :]


def scale_kernel(scale, core_ref, sums_ref, got_ref, gate_ref, up_ref, down_ref):
    share = gate_ref.shape[1]
    half = share // 2
    hidden_width = gate_ref.shape[2]
    core = core_ref[0]

    def put(member, value):
        value = value.astype(F32) * scale
        gate_ref[member] = value[:share]
        up_ref[member] = value[share : 2 * share]
        down_ref[member, :, :hidden_width] = value[2 * share : 2 * share + half]
        down_ref[member, :, hidden_width:] = value[2 * share + half :]

    for c in range(2):

        @pl.when(core == c)
        def _(c=c):
            put(c, sums_ref[c])
            put(1 - c, got_ref[...])


def shards(tokens, out_grad, route_ids, route_gates, w_gate, w_up, w_down):
    dp_size = lax.axis_size("dp")
    expert_size = lax.axis_size("expert")
    members, share, hidden_width = w_gate.shape
    experts = members * expert_size
    chips = dp_size // members
    depth = 3 * share
    token_count, top = route_ids.shape
    width = tokens.shape[1]
    capacity = 5 * token_count * top // (4 * experts)
    slot_count = experts * capacity
    scale = 1.0 / math.sqrt(token_count * dp_size * top / members)
    params = pltpu.CompilerParams(vmem_limit_bytes=VMEM_LIMIT)

    core = lax.rem(lax.axis_index("dp"), members).astype(jnp.int32).reshape(1)
    first = core[0] == 0
    ids, core, first = lax.optimization_barrier((route_ids.T, core, first))
    gates = route_gates.T
    blocks = DISPATCH_STEPS
    block = experts // blocks
    full = lambda *shape: pl.BlockSpec(shape, lambda i: (0,) * len(shape))
    send, slots, packed = pl.pallas_call(
        functools.partial(dispatch_kernel, members, experts),
        grid=(blocks,),
        in_specs=[
            full(*x.shape) for x in (ids, gates, tokens, out_grad, w_gate, w_up, w_down)
        ],
        out_specs=(
            pl.BlockSpec((block, capacity, 2 * width), lambda i: (i, 0, 0)),
            pl.BlockSpec((block * capacity, token_count), lambda i: (i, 0)),
            full(members, depth, hidden_width),
        ),
        out_shape=(
            jax.ShapeDtypeStruct((experts, capacity, 2 * width), BF16),
            jax.ShapeDtypeStruct((slot_count, token_count), BF16),
            jax.ShapeDtypeStruct((members, depth, hidden_width), BF16),
        ),
        scratch_shapes=[pltpu.VMEM((experts, token_count), F32)] * 2,
        compiler_params=params,
        name="dispatch",
    )(ids, gates, tokens, out_grad, w_gate, w_up, w_down)
    weights = lax.all_gather(packed, "dp", axis=0, tiled=False)

    chip_plane = [
        [(chip * members + c) * expert_size + e for c in range(members) for e in range(expert_size)]
        for chip in range(chips)
    ]

    def exchange(x):
        return lax.all_to_all(
            x,
            ("dp", "expert"),
            split_axis=0,
            concat_axis=0,
            tiled=True,
            axis_index_groups=chip_plane,
        )

    recv = exchange(send)

    steps = EXPERT_STEPS
    sources = experts // steps
    rows_count = sources * capacity
    last = steps - 1
    parts, row_grads, gate_rows = pl.pallas_call(
        functools.partial(expert_kernel, steps),
        grid_spec=pltpu.PrefetchScalarGridSpec(
            num_scalar_prefetch=1,
            grid=(steps + 3,),
            in_specs=[
                pl.BlockSpec(
                    (sources, capacity, 2 * width), lambda i, c: (jnp.minimum(i, last), 0, 0)
                ),
                pl.BlockSpec((dp_size, 1, depth, hidden_width), lambda i, c: (0, c[0], 0, 0)),
            ],
            out_specs=(
                pl.BlockSpec(
                    (dp_size, share, hidden_width), lambda i, c: (0, jnp.maximum(i - steps, 0), 0)
                ),
                pl.BlockSpec(
                    (rows_count, 2 * hidden_width), lambda i, c: (jnp.minimum(i, last), 0)
                ),
                pl.BlockSpec((rows_count, LANES), lambda i, c: (jnp.minimum(i, last), 0)),
            ),
            scratch_shapes=[
                pltpu.VMEM((slot_count, width), BF16),
                pltpu.VMEM((slot_count, width), BF16),
                pltpu.VMEM((slot_count, 2 * hidden_width), BF16),
                pltpu.VMEM((slot_count, hidden_width), BF16),
            ],
        ),
        out_shape=(
            jax.ShapeDtypeStruct((dp_size, depth, hidden_width), BF16),
            jax.ShapeDtypeStruct((slot_count, 2 * hidden_width), BF16),
            jax.ShapeDtypeStruct((slot_count, LANES), BF16),
        ),
        compiler_params=params,
        name="expert",
    )(core, recv, weights)
    same_core = [list(range(c, dp_size, members)) for c in range(members)]
    sums = lax.psum_scatter(
        parts.reshape(chips, members, depth, hidden_width),
        "dp",
        scatter_dimension=0,
        tiled=False,
        axis_index_groups=same_core,
    )

    steps = INPUT_STEPS
    sources = experts // steps
    rows_count = sources * capacity
    back = pl.pallas_call(
        input_kernel,
        grid_spec=pltpu.PrefetchScalarGridSpec(
            num_scalar_prefetch=1,
            grid=(steps,),
            in_specs=[
                pl.BlockSpec((rows_count, 2 * hidden_width), lambda i, c: (i, 0)),
                pl.BlockSpec((rows_count, LANES), lambda i, c: (i, 0)),
                pl.BlockSpec((dp_size, 1, 2 * share, hidden_width), lambda i, c: (0, c[0], 0, 0)),
            ],
            out_specs=pl.BlockSpec((sources, capacity, width + LANES), lambda i, c: (i, 0, 0)),
        ),
        out_shape=jax.ShapeDtypeStruct((experts, capacity, width + LANES), BF16),
        compiler_params=params,
        name="inputs",
    )(core, row_grads, gate_rows, weights)
    back, sums = lax.optimization_barrier((exchange(back), sums))
    other = jnp.where(first, sums[1], sums[0])
    got = lax.ppermute(other, "dp", [(i, i ^ 1) for i in range(dp_size)])
    input_grad, gate_grad = pl.pallas_call(
        functools.partial(combine_kernel, members),
        out_shape=(
            jax.ShapeDtypeStruct((token_count, width), BF16),
            jax.ShapeDtypeStruct((top, token_count), F32),
        ),
        compiler_params=params,
        name="combine",
    )(ids, gates, slots, back)

    gate_sum, up_sum, down_sum = pl.pallas_call(
        functools.partial(scale_kernel, scale),
        in_specs=[
            pl.BlockSpec(memory_space=pltpu.SMEM),
            pl.BlockSpec(memory_space=pltpu.VMEM),
            pl.BlockSpec(memory_space=pltpu.VMEM),
        ],
        out_shape=tuple(jax.ShapeDtypeStruct(w.shape, F32) for w in (w_gate, w_up, w_down)),
        compiler_params=params,
        name="scale",
    )(core, sums, got)
    return (input_grad, gate_grad.T, gate_sum, up_sum, down_sum)


def solution(mesh):
    return jax.shard_map(
        shards,
        mesh=mesh,
        in_specs=(
            P(("dp", "expert"), None),
            P(("dp", "expert"), None),
            P(("dp", "expert"), None),
            P(("dp", "expert"), None),
            P("expert", "dp", None),
            P("expert", "dp", None),
            P("expert", "dp", None),
        ),
        out_specs=(
            P(("dp", "expert"), None),
            P(("dp", "expert"), None),
            P("expert", "dp", None),
            P("expert", "dp", None),
            P("expert", "dp", None),
        ),
        check_vma=False,
    )
```

time: 187 us -> 163 us (0.87)
  waiting for transfers between devices: 82.8 us -> 0.04 us
  blocking collectives: 42.1 us -> 113 us
  starting transfers between devices: 9.54 us -> 1.41 us
  other arithmetic: 4.65 us -> 1.04 us
    all_to_all x1 -> x0, waiting for transfers between devices: 77.3 us -> none  [shards(): lax.all_to_all(send, 'expert', split_axis=0, concat_axis=0, tiled=True)]
    all_to_all x1 -> x2, blocking collectives: 42.1 us -> 113 us  [exchange(): lax.all_to_all(x, ('dp', 'expert'), split_axis=0, concat_axis=0, tiled=Tr...]
    all_to_all x1 -> x0, starting transfers between devices: 7.66 us -> none  [shards(): lax.all_to_all(send, 'expert', split_axis=0, concat_axis=0, tiled=True)]
    ppermute x1, waiting for transfers between devices: 5.5 us -> 0.01 us  [shards(): got = lax.ppermute(other, 'dp', [(i, i ^ 1) for i in range(dp_size)])]
    add x1 -> x0, other arithmetic: 4.65 us -> none  [shards(): pair_sum = keep + got]
  transfers between devices with their start and end apart: 4 -> 3, of which waited for: 2 -> 0; matrix products, arithmetic and copies ran while one was open for 0% -> 0% of each run, Pallas kernels for 5% -> 6%
where the time goes in v3:
time: 163 us; the launch traced here: 162 us
  blocking collectives  113 us (69%)
  Pallas kernels  31.7 us (19%)
  between operations  14.1 us (9%)
    all_to_all x2, blocking collectives, exchange(): lax.all_to_all(x, ('dp', 'expert'), split_axis=0, concat_axis=0, tiled=Tr...  113 us
    pallas_call x1, Pallas kernels, shards(): pl.pallas_call(functools.partial(expert_kernel, steps), grid_spec=pltpu.P...  14.5 us
    pallas_call x1, Pallas kernels, shards(): pl.pallas_call(input_kernel, grid_spec=pltpu.PrefetchScalarGridSpec(num_s...  6.9 us
    pallas_call x1, Pallas kernels, shards(): pl.pallas_call(functools.partial(dispatch_kernel, members, experts), grid...  5.08 us
  transfers between devices with their start and end apart: 3, of which 0 were waited for; matrix products, arithmetic and copies ran while one was open for 0% of the time, Pallas kernels for 6%

profile of v3, /device:TPU:1, one launch (start us, length us, event | category | flops | bytes accessed | tf_op | source)
XLA Modules:
  0.0 162.1 jit_solution(12794575570843326619)
XLA Ops:
  7.2 0.0 all-gather.3.cloned.1.call-start
  7.2 5.1 %dispatch.1 = (bf16[32,40,2048]{2,1,0:T(8,128)(2,1)}, bf16[1280,128]{1,0:T(8,128)(2,1)}, bf16[2,192,512]{2,1,0:T(8,128)(2,1)}) custom-call(s32[8,128]{1,0:T(8,128)} %bitcast.14, f32[8,128]{1,0:T(8,128)} %bitcast.16, bf16[128,1024]{1,0:T(8,128)(2,1)} %tokens_ref.1, bf16[128,1024]{1,0:T(8,128)(2,1)} %grads_ref.1, bf16[2,64,512]{2,1,0:T(8,128)(2,1)} %w_gate_ref.1, ...), custom_call_target="tpu_custom_call" | custom-call | tf_op jit(solution)/shard_map/dispatch/pallas_call | solution.py:237
  12.3 0.0 all-gather.3.cloned.1.call-update
  12.3 0.0 reduce-scatter.2.cloned.1.call-start
  12.4 70.2 %all_to_all.10.recv_ref = bf16[32,40,2048]{2,1,0:T(8,128)(2,1)} all-to-all(bf16[32,40,2048]{2,1,0:T(8,128)(2,1)} %get-tuple-element.24), channel_id=1, replica_groups={{0,1,2,3,4,5,6,7,8,9,10,11,12,13,14,15,16,17,18,19,20,21,22,23,24,25,26..., dimensions={0} | all-to-all | bytes 10485760 | tf_op jit(solution)/shard_map/all_to_all | solution.py:265
  82.6 0.0 all-gather.3.cloned.1.call-done
  82.6 14.5 %expert.1 = (bf16[16,192,512]{2,1,0:T(8,128)(2,1)}, bf16[1280,1024]{1,0:T(8,128)(2,1)}, bf16[1280,128]{1,0:T(8,128)(2,1)}) custom-call(s32[1]{0:T(128)} %bitcast.1.core_ref, bf16[32,40,2048]{2,1,0:T(8,128)(2,1)} %all_to_all.10.recv_ref, bf16[16,2,192,512]{3,2,1,0:T(8,128)(2,1)} %bitcast.9), custom_call_target="tpu_custom_call" | custom-call | tf_op jit(solution)/shard_map/expert/pallas_call | solution.py:280
  97.0 0.0 reduce-scatter.2.cloned.1.call-update
  97.1 6.9 %inputs.1 = bf16[32,40,1152]{2,1,0:T(8,128)(2,1)} custom-call(s32[1]{0:T(128)} %bitcast.1.core_ref, bf16[1280,1024]{1,0:T(8,128)(2,1)} %get-tuple-element.26.grads_ref, bf16[1280,128]{1,0:T(8,128)(2,1)} %get-tuple-element.27.gate_ref, bf16[16,2,192,512]{3,2,1,0:T(8,128)(2,1)} %bitcast.10), custom_call_target="tpu_custom_call" | custom-call | tf_op jit(solution)/shard_map/inputs/pallas_call | solution.py:327
  104.0 43.0 %all_to_all.11.back_ref = bf16[32,40,1152]{2,1,0:T(8,128)(2,1)} all-to-all(bf16[32,40,1152]{2,1,0:T(8,128)(2,1)} %inputs.1), channel_id=1, replica_groups={{0,1,2,3,4,5,6,7,8,9,10,11,12,13,14,15,16,17,18,19,20,21,22,23,24,25,26..., dimensions={0} | all-to-all | bytes 5898240 | tf_op jit(solution)/shard_map/all_to_all | solution.py:265
  147.0 0.0 reduce-scatter.2.cloned.1.call-done
  147.0 1.0 select_bitcast_fusion
  148.1 1.3 collective-permute-start
  149.4 3.2 %combine.1 = (bf16[128,1024]{1,0:T(8,128)(2,1)}, f32[8,128]{1,0:T(8,128)}) custom-call(s32[8,128]{1,0:T(8,128)} %bitcast.15, f32[8,128]{1,0:T(8,128)} %bitcast.17, bf16[1280,128]{1,0:T(8,128)(2,1)} %get-tuple-element.22.slots_ref, bf16[32,40,1152]{2,1,0:T(8,128)(2,1)} %all_to_all.11.back_ref), custom_call_target="tpu_custom_call" | custom-call | tf_op jit(solution)/shard_map/combine/pallas_call | solution.py:346
  152.6 0.0 collective-permute-done.got_ref
  152.6 0.0 copy-start
  152.6 0.7 copy-done
  153.3 2.0 %scale.1 = (f32[2,64,512]{2,1,0:T(8,128)}, f32[2,64,512]{2,1,0:T(8,128)}, f32[2,32,1024]{2,1,0:T(8,128)}) custom-call(s32[1]{0:T(128)} %bitcast.1.core_ref, bf16[2,192,512]{2,1,0:T(8,128)(2,1)} %bitcast.13, bf16[192,512]{1,0:T(8,128)(2,1)} %copy-done), custom_call_target="tpu_custom_call" | custom-call | tf_op jit(solution)/shard_map/scale/pallas_call | solution.py:356
Async XLA Ops:
  7.2 75.4 %all-gather.3.cloned.1.call-start = ((), (), s32[]{:S(2)}) async-start(), calls=%async_computation.4 | async-start | bytes 6684672 | tf_op jit(solution)/shard_map/all_gather | solution.py:257
  12.3 134.7 %reduce-scatter.2.cloned.1.call-start = ((), (), s32[]{:S(2)}) async-start(), calls=%async_computation.3 | async-start | bytes 3538944 | tf_op jit(solution)/shard_map/reduce_scatter | solution.py:316
  148.1 4.6 %collective-permute-start = (bf16[192,512]{1,0:T(8,128)(2,1)S(1)}, bf16[192,512]{1,0:T(8,128)(2,1)S(1)}, u32[]{:S(2)}, u32[]{:S(2)}) collective-permute-start(bf16[192,512]{1,0:T(8,128)(2,1)S(1)} %select_bitcast_fusion), channel_id=1, source_target_pairs={{0,16},{16,0},{32,48},{48,32},{64,80},{80,64},{96,112},{112,96},{1... | collective-permute-start | bytes 589832 | tf_op jit(solution)/shard_map/ppermute | solution.py:345
  152.6 0.7 copy-start
Sparse Core Ops, SparseCore 0:
  12.4 50.2 all-gather.2
  97.2 43.7 reduce-scatter.1

commit v4 on v3

v4 whole, which is shorter than its diff:
```python
import functools
import math

import jax
import jax.numpy as jnp
from jax import lax
from jax.experimental import pallas as pl
from jax.experimental.pallas import tpu as pltpu
from jax.sharding import PartitionSpec as P

F32 = jnp.float32
BF16 = jnp.bfloat16
MIB = 1024 * 1024
TILE = 8
PANEL = 256
CHUNKS = 4


def in_vmem(x):
    return pltpu.with_memory_space_constraint(x, pltpu.VMEM)


def in_hbm(x):
    return pltpu.with_memory_space_constraint(x, pltpu.HBM)


def vmem_result(*shape):
    return pltpu.VMEM(shape, BF16)


def hbm_result(*shape):
    return pltpu.HBM(shape, BF16)


def dot(a, b, ca, cb):
    return lax.dot_general(a, b, (((ca,), (cb,)), ((), ())), preferred_element_type=F32)


def split_high_low(x):
    high = x.astype(BF16)
    return high, (x - high.astype(F32)).astype(BF16)


def expert_of_row(shape, members):
    row = lax.broadcasted_iota(jnp.int32, shape, 0)
    per_member = shape[0] // members
    return lax.rem(row, per_member) * members + row // per_member


def weight_copies(gate_ref, up_ref, down_ref, packed_ref, sems):
    share = gate_ref.shape[1]
    half = share // 2
    hidden_width = gate_ref.shape[2]
    pieces = (
        (gate_ref, 0, share),
        (up_ref, share, share),
        (down_ref.at[:, :, :hidden_width], 2 * share, half),
        (down_ref.at[:, :, hidden_width:], 2 * share + half, half),
    )
    return [
        pltpu.make_async_copy(ref, packed_ref.at[:, start : start + size, :], sems.at[k])
        for k, (ref, start, size) in enumerate(pieces)
    ]


def dispatch_kernel(
    members,
    ids_ref,
    gates_ref,
    tokens_ref,
    grads_ref,
    w_gate_ref,
    w_up_ref,
    w_down_ref,
    send_ref,
    slots_ref,
    packed_ref,
    tokens_buf,
    grads_buf,
    send_buf,
    weight_sems,
    token_sems,
    send_sems,
):
    loads = [
        pltpu.make_async_copy(tokens_ref, tokens_buf, token_sems.at[0]),
        pltpu.make_async_copy(grads_ref, grads_buf, token_sems.at[1]),
    ]
    for copy in loads:
        copy.start()
    packing = weight_copies(w_gate_ref, w_up_ref, w_down_ref, packed_ref, weight_sems)
    for copy in packing:
        copy.start()
    experts, capacity, _ = send_buf.shape
    token_count, width = tokens_buf.shape
    ids = ids_ref[...]
    expert = expert_of_row((experts, token_count), members)
    named = jnp.zeros((experts, token_count), F32)
    gates = jnp.zeros((experts, token_count), F32)
    for k in range(ids.shape[0]):
        same = ids[k : k + 1, :] == expert
        named = named + jnp.where(same, 1.0, 0.0)
        gates = gates + jnp.where(same, gates_ref[k : k + 1, :], 0.0)
    earlier = lax.broadcasted_iota(jnp.int32, (token_count, token_count), 0)
    later = lax.broadcasted_iota(jnp.int32, (token_count, token_count), 1)
    before = jnp.where(earlier < later, 1.0, 0.0).astype(BF16)
    ranks = dot(named.astype(BF16), before, 1, 0)
    keys = jnp.where(named > 0.0, ranks, -1.0)
    for copy in loads:
        copy.wait()
    tokens = tokens_buf[...]
    grads = jnp.concatenate([grads_buf[...], grads_buf[...]], axis=0)
    block = experts // CHUNKS
    count = block * capacity
    place = lax.broadcasted_iota(jnp.int32, (block, capacity, token_count), 1).astype(F32)
    sends = []
    for i in range(CHUNKS):
        start = i * block
        hit = keys[start : start + block, None, :] == place
        slots = jnp.where(hit, 1.0, 0.0).reshape(count, token_count).astype(BF16)
        slots_ref[i * count : (i + 1) * count, :] = slots
        weighted = jnp.where(hit, gates[start : start + block, None, :], 0.0)
        high, low = split_high_low(weighted.reshape(count, token_count))
        rows = dot(slots, tokens, 1, 0)
        scaled = dot(jnp.concatenate([high, low], axis=1), grads, 1, 0)
        shape = (block, capacity, width)
        here = slice(start, start + block)
        send_buf[here, :, :width] = rows.astype(BF16).reshape(shape)
        send_buf[here, :, width:] = scaled.astype(BF16).reshape(shape)
        sends.append(
            pltpu.make_async_copy(send_buf.at[here], send_ref.at[here], send_sems.at[i])
        )
        sends[i].start()
    for copy in packing + sends:
        copy.wait()


def expert_kernel(
    core_ref,
    recv_ref,
    weights_ref,
    parts_ref,
    grads_ref,
    gate_ref,
    ins_ref,
    rows_ref,
    down_ref,
    hidden_ref,
    stage_ref,
    row_sems,
    in_sems,
    out_sems,
):
    sources, capacity, _ = rows_ref.shape
    pieces, _, depth, hidden_width = weights_ref.shape
    share = depth // 3
    half = share // 2
    slot_count = sources * capacity
    width = pieces * share
    core = core_ref[0]

    def fetch(k, target):
        return pltpu.make_async_copy(
            weights_ref.at[:, core, k * share : (k + 1) * share, :], target, in_sems.at[k]
        )

    fetches = [
        fetch(0, ins_ref.at[:, :, :hidden_width]),
        fetch(1, ins_ref.at[:, :, hidden_width:]),
        fetch(2, down_ref),
    ]
    block = sources // CHUNKS
    arrivals = [
        pltpu.make_async_copy(
            recv_ref.at[i * block : (i + 1) * block],
            rows_ref.at[i * block : (i + 1) * block],
            row_sems.at[i],
        )
        for i in range(CHUNKS)
    ]
    fetches[0].start()
    arrivals[0].start()
    fetches[1].start()
    fetches[2].start()
    fetches[0].wait()
    arrivals[0].wait()
    for copy in arrivals[1:]:
        copy.start()
    fetches[1].wait()
    fetches[2].wait()
    w_gate = ins_ref[:, :, :hidden_width].reshape(width, hidden_width)
    w_up = ins_ref[:, :, hidden_width:].reshape(width, hidden_width)
    down = jnp.concatenate(
        [
            down_ref[:, :half, :].reshape(hidden_width, hidden_width),
            down_ref[:, half:, :].reshape(hidden_width, hidden_width),
        ],
        axis=1,
    )
    count = block * capacity
    tiles = capacity // TILE
    lane = lax.broadcasted_iota(jnp.int32, (block, TILE, PANEL), 2)
    for i in range(CHUNKS):
        here = slice(i * block, (i + 1) * block)
        where = slice(i * count, (i + 1) * count)
        if i > 0:
            arrivals[i].wait()
        rows = rows_ref[here, :, :width].reshape(count, width)
        scaled = rows_ref[here, :, width:].reshape(count, width)
        gate_pre = dot(rows, w_gate, 1, 0)
        up_proj = dot(rows, w_up, 1, 0)
        hidden_grad = dot(scaled, down, 1, 1)
        sig = jax.nn.sigmoid(gate_pre)
        act = gate_pre * sig
        hidden = (act * up_proj).astype(BF16)
        hidden_ref[where, :] = hidden
        grads_ref[where, hidden_width:] = (hidden_grad * act).astype(BF16)
        pre_grad = hidden_grad * up_proj * (sig * (1.0 + gate_pre * (1.0 - sig)))
        grads_ref[where, :hidden_width] = pre_grad.astype(BF16)
        gate_grad = jnp.sum(hidden.astype(F32) * hidden_grad, axis=1, keepdims=True)
        gate_grad = gate_grad.reshape(block, tiles, TILE, 1)
        tile = jnp.zeros((block, TILE, PANEL), F32)
        for n in range(tiles):
            value = jnp.broadcast_to(gate_grad[:, n], (block, TILE, PANEL))
            high, low = split_high_low(value)
            tile = jnp.where(lane == 2 * n, high.astype(F32), tile)
            tile = jnp.where(lane == 2 * n + 1, low.astype(F32), tile)
        gate_ref[here] = tile.astype(BF16)

    def store(k):
        return pltpu.make_async_copy(
            stage_ref.at[k], parts_ref.at[:, k * share : (k + 1) * share, :], out_sems.at[k]
        )

    stores = [store(k) for k in range(3)]
    rows = rows_ref[:, :, :width].reshape(slot_count, width)
    for k in range(2):
        own = grads_ref[:, k * hidden_width : (k + 1) * hidden_width]
        total = dot(rows, own, 0, 0).astype(BF16)
        stage_ref[k] = total.reshape(pieces, share, hidden_width)
        stores[k].start()
    scaled = rows_ref[:, :, width:].reshape(slot_count, width)
    total = dot(hidden_ref[...], scaled, 0, 0).astype(BF16)
    stage_ref[2, :, :half, :] = total[:, :hidden_width].reshape(pieces, half, hidden_width)
    stage_ref[2, :, half:, :] = total[:, hidden_width:].reshape(pieces, half, hidden_width)
    stores[2].start()
    for copy in stores:
        copy.wait()


def input_kernel(core_ref, grads_ref, gate_ref, weights_ref, back_ref, ins_ref, sems):
    sources, panels, _, _ = back_ref.shape
    share = weights_ref.shape[2] // 3
    pieces, hidden_width = ins_ref.shape[0], ins_ref.shape[2] // 2
    core = core_ref[0]
    span = PANEL // share
    loads = []
    for n in range(pieces // span):
        here = slice(n * span, (n + 1) * span)
        for k in range(2):
            loads.append(
                pltpu.make_async_copy(
                    weights_ref.at[here, core, k * share : (k + 1) * share, :],
                    ins_ref.at[here, :, k * hidden_width : (k + 1) * hidden_width],
                    sems.at[n, k],
                )
            )
    for copy in loads:
        copy.start()
    back_ref[:, panels - 1] = gate_ref[...]
    grads = grads_ref[...]
    tiles = (panels - 1) * span // pieces
    for n in range(pieces // span):
        loads[2 * n].wait()
        loads[2 * n + 1].wait()
        weights = ins_ref[n * span : (n + 1) * span].reshape(PANEL, 2 * hidden_width)
        panel = dot(grads, weights, 1, 1).astype(BF16)
        back_ref[:, n * tiles : (n + 1) * tiles] = panel.reshape(sources, tiles, TILE, PANEL)


def combine_kernel(members, ids_ref, gates_ref, slots_ref, back_ref, input_ref, gate_ref):
    experts, panels, _, _ = back_ref.shape
    top, token_count = ids_ref.shape
    width = input_ref.shape[1]
    slot_count = slots_ref.shape[0]
    tiles = slot_count // (experts * TILE)
    slots = slots_ref[...]
    for n in range(width // PANEL):
        rows = back_ref[:, n * tiles : (n + 1) * tiles].reshape(slot_count, PANEL)
        input_ref[:, n * PANEL : (n + 1) * PANEL] = dot(slots, rows, 0, 0).astype(BF16)
    extra = back_ref[:, panels - 1].astype(F32)
    hits = slots.astype(F32).reshape(experts, tiles * TILE, token_count)
    by_expert = jnp.zeros((experts, token_count), F32)
    for n in range(tiles):
        value = extra[:, :, 2 * n : 2 * n + 1] + extra[:, :, 2 * n + 1 : 2 * n + 2]
        picked = jnp.where(hits[:, n * TILE : (n + 1) * TILE, :] > 0.0, value, 0.0)
        by_expert = by_expert + jnp.sum(picked, axis=1)
    expert = expert_of_row((experts, token_count), members)
    ids = ids_ref[...]
    for k in range(top):
        own = jnp.where(ids[k : k + 1, :] == expert, by_expert, 0.0)
        gate_ref[k : k + 1, :] = jnp.sum(own, axis=0, keepdims=True) / gates_ref[k : k + 1, :]


def scale_kernel(scale, core_ref, sums_ref, got_ref, gate_ref, up_ref, down_ref):
    share = gate_ref.shape[1]
    half = share // 2
    hidden_width = gate_ref.shape[2]
    core = core_ref[0]

    def put(member, value):
        value = value.astype(F32) * scale
        gate_ref[member] = value[:share]
        up_ref[member] = value[share : 2 * share]
        down_ref[member, :, :hidden_width] = value[2 * share : 2 * share + half]
        down_ref[member, :, hidden_width:] = value[2 * share + half :]

    for c in range(2):

        @pl.when(core == c)
        def _(c=c):
            put(c, sums_ref[c])
            put(1 - c, got_ref[...])


def shards(tokens, out_grad, route_ids, route_gates, w_gate, w_up, w_down):
    dp_size = lax.axis_size("dp")
    expert_size = lax.axis_size("expert")
    members, share, hidden_width = w_gate.shape
    experts = members * expert_size
    chips = dp_size // members
    depth = 3 * share
    token_count, top = route_ids.shape
    width = tokens.shape[1]
    capacity = 5 * token_count * top // (4 * experts)
    slot_count = experts * capacity
    scale = 1.0 / math.sqrt(token_count * dp_size * top / members)
    params = lambda mib: pltpu.CompilerParams(vmem_limit_bytes=mib * MIB)
    vmem = pl.BlockSpec(memory_space=pltpu.VMEM)
    smem = pl.BlockSpec(memory_space=pltpu.SMEM)
    anywhere = pl.BlockSpec(memory_space=pl.ANY)

    core = lax.rem(lax.axis_index("dp"), members).astype(jnp.int32).reshape(1)
    first = core[0] == 0
    ids, core, first = lax.optimization_barrier((route_ids.T, core, first))
    gates = route_gates.T
    send, slots, packed = pl.pallas_call(
        functools.partial(dispatch_kernel, members),
        in_specs=[vmem, vmem] + [anywhere] * 5,
        out_specs=(anywhere, vmem, anywhere),
        out_shape=(
            hbm_result(experts, capacity, 2 * width),
            vmem_result(slot_count, token_count),
            hbm_result(members, depth, hidden_width),
        ),
        scratch_shapes=[
            pltpu.VMEM((token_count, width), BF16),
            pltpu.VMEM((token_count, width), BF16),
            pltpu.VMEM((experts, capacity, 2 * width), BF16),
            pltpu.SemaphoreType.DMA((4,)),
            pltpu.SemaphoreType.DMA((2,)),
            pltpu.SemaphoreType.DMA((CHUNKS,)),
        ],
        compiler_params=params(24),
        name="dispatch",
    )(in_hbm(ids), in_hbm(gates), *map(in_hbm, (tokens, out_grad, w_gate, w_up, w_down)))
    weights = lax.all_gather(packed, "dp", axis=0, tiled=False)

    chip_plane = [
        [(chip * members + c) * expert_size + e for c in range(members) for e in range(expert_size)]
        for chip in range(chips)
    ]

    def exchange(x):
        return lax.all_to_all(
            x,
            ("dp", "expert"),
            split_axis=0,
            concat_axis=0,
            tiled=True,
            axis_index_groups=chip_plane,
        )

    recv = exchange(send)

    parts, row_grads, gate_tiles = pl.pallas_call(
        expert_kernel,
        in_specs=[smem, anywhere, anywhere],
        out_specs=(anywhere, vmem, vmem),
        out_shape=(
            hbm_result(dp_size, depth, hidden_width),
            vmem_result(slot_count, 2 * hidden_width),
            vmem_result(experts, TILE, PANEL),
        ),
        scratch_shapes=[
            pltpu.VMEM((dp_size, share, 2 * hidden_width), BF16),
            pltpu.VMEM((experts, capacity, 2 * width), BF16),
            pltpu.VMEM((dp_size, share, hidden_width), BF16),
            pltpu.VMEM((slot_count, hidden_width), BF16),
            pltpu.VMEM((3, dp_size, share, hidden_width), BF16),
            pltpu.SemaphoreType.DMA((CHUNKS,)),
            pltpu.SemaphoreType.DMA((3,)),
            pltpu.SemaphoreType.DMA((3,)),
        ],
        compiler_params=params(40),
        name="expert",
    )(core, in_hbm(recv), in_hbm(weights))
    same_core = [list(range(c, dp_size, members)) for c in range(members)]
    sums = lax.psum_scatter(
        parts.reshape(chips, members, depth, hidden_width),
        "dp",
        scatter_dimension=0,
        tiled=False,
        axis_index_groups=same_core,
    )

    panels = capacity * width // (TILE * PANEL) + 1
    back = pl.pallas_call(
        input_kernel,
        in_specs=[smem, vmem, vmem, anywhere],
        out_specs=vmem,
        out_shape=vmem_result(experts, panels, TILE, PANEL),
        scratch_shapes=[
            pltpu.VMEM((dp_size, share, 2 * hidden_width), BF16),
            pltpu.SemaphoreType.DMA((width // PANEL, 2)),
        ],
        compiler_params=params(24),
        name="inputs",
    )(core, in_vmem(row_grads), in_vmem(gate_tiles), in_hbm(weights))
    back, sums = lax.optimization_barrier((exchange(back), sums))
    other = jnp.where(first, sums[1], sums[0])
    got = lax.ppermute(other, "dp", [(i, i ^ 1) for i in range(dp_size)])
    input_grad, gate_grad = pl.pallas_call(
        functools.partial(combine_kernel, members),
        out_shape=(
            jax.ShapeDtypeStruct((token_count, width), BF16),
            jax.ShapeDtypeStruct((top, token_count), F32),
        ),
        compiler_params=params(24),
        name="combine",
    )(ids, gates, in_vmem(slots), in_vmem(back))

    gate_sum, up_sum, down_sum = pl.pallas_call(
        functools.partial(scale_kernel, scale),
        in_specs=[smem, vmem, vmem],
        out_shape=tuple(jax.ShapeDtypeStruct(w.shape, F32) for w in (w_gate, w_up, w_down)),
        compiler_params=params(16),
        name="scale",
    )(core, sums, in_vmem(got))
    return (input_grad, gate_grad.T, gate_sum, up_sum, down_sum)


def solution(mesh):
    return jax.shard_map(
        shards,
        mesh=mesh,
        in_specs=(
            P(("dp", "expert"), None),
            P(("dp", "expert"), None),
            P(("dp", "expert"), None),
            P(("dp", "expert"), None),
            P("expert", "dp", None),
            P("expert", "dp", None),
            P("expert", "dp", None),
        ),
        out_specs=(
            P(("dp", "expert"), None),
            P(("dp", "expert"), None),
            P("expert", "dp", None),
            P("expert", "dp", None),
            P("expert", "dp", None),
        ),
        check_vma=False,
    )
```

time: 163 us -> 162 us (level)
  Pallas kernels: 31.7 us -> 36.2 us
  blocking collectives: 113 us -> 109 us
    pallas_call x4, Pallas kernels: 28.4 us -> 34.9 us  [the longest x1 13.8 us: shards(): pl.pallas_call(functools.partial(dispatch_kernel, members), in_specs=[vme...]
    all_to_all x2, blocking collectives: 113 us -> 109 us  [exchange(): lax.all_to_all(x, ('dp', 'expert'), split_axis=0, concat_axis=0, tiled=Tr...]
    pallas_call x1, Pallas kernels: 3.24 us -> 1.27 us  [shards(): pl.pallas_call(functools.partial(combine_kernel, members), out_shape=(jax...]
  transfers between devices with their start and end apart: 3 -> 3, of which waited for: 0 -> 0; matrix products, arithmetic and copies ran while one was open for 0% -> 0% of each run, Pallas kernels for 6% -> 5%
where the time goes in v4:
time: 162 us
  blocking collectives  109 us (67%)
  Pallas kernels  36.2 us (22%)
  between operations  14.1 us (9%)
    all_to_all x2, blocking collectives, exchange(): lax.all_to_all(x, ('dp', 'expert'), split_axis=0, concat_axis=0, tiled=Tr...  109 us
    pallas_call x1, Pallas kernels, shards(): pl.pallas_call(functools.partial(dispatch_kernel, members), in_specs=[vme...  13.8 us
    pallas_call x1, Pallas kernels, shards(): pl.pallas_call(expert_kernel, in_specs=[smem, anywhere, anywhere], out_sp...  12.9 us
    pallas_call x1, Pallas kernels, shards(): pl.pallas_call(input_kernel, in_specs=[smem, vmem, vmem, anywhere], out_s...  7.28 us
  transfers between devices with their start and end apart: 3, of which 0 were waited for; matrix products, arithmetic and copies ran while one was open for 0% of the time, Pallas kernels for 5%

profile of v4, /device:TPU:1, one launch (start us, length us, event | category | flops | bytes accessed | tf_op | source)
XLA Modules:
  0.0 162.1 jit_solution(9010479365742552591)
XLA Ops:
  7.2 0.0 all-gather.3.cloned.1.call-start
  7.2 13.8 %dispatch.1 = (bf16[32,40,2048]{2,1,0:T(8,128)(2,1)}, bf16[1280,128]{1,0:T(8,128)(2,1)S(1)}, bf16[2,192,512]{2,1,0:T(8,128)(2,1)}) custom-call(s32[8,128]{1,0:T(8,128)} %bitcast.11, f32[8,128]{1,0:T(8,128)} %bitcast.13, bf16[128,1024]{1,0:T(8,128)(2,1)} %tokens_ref.1, bf16[128,1024]{1,0:T(8,128)(2,1)} %grads_ref.1, bf16[2,64,512]{2,1,0:T(8,128)(2,1)} %w_gate_ref.1, ...), custom_call_target="tpu_custom_call" | custom-call | tf_op jit(solution)/shard_map/dispatch/pallas_call | solution.py:347
  21.0 0.0 all-gather.3.cloned.1.call-update
  21.1 0.0 reduce-scatter.2.cloned.1.call-start
  21.1 70.2 %all_to_all.10.recv_ref = bf16[32,40,2048]{2,1,0:T(8,128)(2,1)} all-to-all(bf16[32,40,2048]{2,1,0:T(8,128)(2,1)} %get-tuple-element.24), channel_id=1, replica_groups={{0,1,2,3,4,5,6,7,8,9,10,11,12,13,14,15,16,17,18,19,20,21,22,23,24,25,26..., dimensions={0} | all-to-all | bytes 10485760 | tf_op jit(solution)/shard_map/all_to_all | solution.py:375
  91.3 0.0 all-gather.3.cloned.1.call-done
  91.3 12.9 %expert.1 = (bf16[16,192,512]{2,1,0:T(8,128)(2,1)}, bf16[1280,1024]{1,0:T(8,128)(2,1)S(1)}, bf16[32,8,256]{2,1,0:T(8,128)(2,1)S(1)}) custom-call(s32[1]{0:T(128)} %bitcast.1.core_ref, bf16[32,40,2048]{2,1,0:T(8,128)(2,1)} %all_to_all.10.recv_ref, bf16[16,2,192,512]{3,2,1,0:T(8,128)(2,1)} %bitcast.15), custom_call_target="tpu_custom_call" | custom-call | tf_op jit(solution)/shard_map/expert/pallas_call | solution.py:386
  104.2 0.0 reduce-scatter.2.cloned.1.call-update
  104.2 7.3 %inputs.1 = bf16[32,21,8,256]{3,2,1,0:T(8,128)(2,1)S(1)} custom-call(s32[1]{0:T(128)} %bitcast.1.core_ref, bf16[1280,1024]{1,0:T(8,128)(2,1)S(1)} %get-tuple-element.26.grads_ref, bf16[32,8,256]{2,1,0:T(8,128)(2,1)S(1)} %get-tuple-element.27.gate_ref, bf16[16,2,192,512]{3,2,1,0:T(8,128)(2,1)} %bitcast.16), custom_call_target="tpu_custom_call" | custom-call | tf_op jit(solution)/shard_map/inputs/pallas_call | solution.py:418
  111.5 0.0 copy-start.1
  111.6 0.0 copy-start.2
  111.6 39.0 %all_to_all.11.back_ref = bf16[32,21,8,256]{3,2,1,0:T(8,128)(2,1)S(1)} all-to-all(bf16[32,21,8,256]{3,2,1,0:T(8,128)(2,1)S(1)} %inputs.1), channel_id=1, replica_groups={{0,1,2,3,4,5,6,7,8,9,10,11,12,13,14,15,16,17,18,19,20,21,22,23,24,25,26..., dimensions={0} | all-to-all | bytes 5505024 | tf_op jit(solution)/shard_map/all_to_all | solution.py:375
  150.6 0.0 reduce-scatter.2.cloned.1.call-done
  150.6 0.0 copy-start
  150.6 1.1 select_bitcast_fusion
  151.7 1.3 collective-permute-start
  153.0 0.0 copy-done.1
  153.0 0.0 copy-done.2
  153.0 1.3 combine.1
  154.3 0.0 collective-permute-done.got_ref
  154.3 0.0 copy-done
  154.3 0.9 scale.1
Async XLA Ops:
  7.2 84.1 %all-gather.3.cloned.1.call-start = ((), (), s32[]{:S(2)}) async-start(), calls=%async_computation.4 | async-start | bytes 6684672 | tf_op jit(solution)/shard_map/all_gather | solution.py:367
  21.1 129.5 %reduce-scatter.2.cloned.1.call-start = ((), (), s32[]{:S(2)}) async-start(), calls=%async_computation.3 | async-start | bytes 3538944 | tf_op jit(solution)/shard_map/reduce_scatter | solution.py:409
  111.5 41.5 %copy-start.1 = (s32[128,8]{0,1:T(8,128)S(1)}, s32[128,8]{0,1:T(8,128)}, u32[]{:S(2)}) copy-start(s32[128,8]{0,1:T(8,128)} %param.9) | copy-start | bytes 12292
  111.6 41.5 %copy-start.2 = (f32[128,8]{0,1:T(8,128)S(1)}, f32[128,8]{0,1:T(8,128)}, u32[]{:S(2)}) copy-start(f32[128,8]{0,1:T(8,128)} %param.10) | copy-start | bytes 12292
  150.6 3.7 %copy-start = (bf16[1,2,192,512]{3,2,1,0:T(8,128)(2,1)S(1)}, bf16[1,2,192,512]{3,2,1,0:T(8,128)(2,1)}, u32[]{:S(2)}) copy-start(bf16[1,2,192,512]{3,2,1,0:T(8,128)(2,1)} %reduce-scatter.2.cloned.1.call-done) | copy-start | bytes 1179652
  151.7 2.6 %collective-permute-start = (bf16[192,512]{1,0:T(8,128)(2,1)S(1)}, bf16[192,512]{1,0:T(8,128)(2,1)S(1)}, u32[]{:S(2)}, u32[]{:S(2)}) collective-permute-start(bf16[192,512]{1,0:T(8,128)(2,1)S(1)} %select_bitcast_fusion), channel_id=1, source_target_pairs={{0,16},{16,0},{32,48},{48,32},{64,80},{80,64},{96,112},{112,96},{1... | collective-permute-start | bytes 589832 | tf_op jit(solution)/shard_map/ppermute | solution.py:432
Sparse Core Ops, SparseCore 0:
  21.2 50.2 all-gather.2
  104.4 43.8 reduce-scatter.1

commit v5 on v4

--- a/solution.py
+++ b/solution.py
@@ -47,7 +47,7 @@
     return lax.rem(row, per_member) * members + row // per_member
 
 
-def weight_copies(gate_ref, up_ref, down_ref, packed_ref, sems):
+def weight_copies(gate_ref, up_ref, down_ref, packed_buf, sems):
     share = gate_ref.shape[1]
     half = share // 2
     hidden_width = gate_ref.shape[2]
@@ -58,7 +58,7 @@
         (down_ref.at[:, :, hidden_width:], 2 * share + half, half),
     )
     return [
-        pltpu.make_async_copy(ref, packed_ref.at[:, start : start + size, :], sems.at[k])
+        pltpu.make_async_copy(ref, packed_buf.at[:, start : start + size, :], sems.at[k])
         for k, (ref, start, size) in enumerate(pieces)
     ]
 
@@ -78,6 +78,7 @@
     tokens_buf,
     grads_buf,
     send_buf,
+    packed_buf,
     weight_sems,
     token_sems,
     send_sems,
@@ -88,7 +89,7 @@
     ]
     for copy in loads:
         copy.start()
-    packing = weight_copies(w_gate_ref, w_up_ref, w_down_ref, packed_ref, weight_sems)
+    packing = weight_copies(w_gate_ref, w_up_ref, w_down_ref, packed_buf, weight_sems)
     for copy in packing:
         copy.start()
     experts, capacity, _ = send_buf.shape
@@ -106,8 +107,10 @@
     before = jnp.where(earlier < later, 1.0, 0.0).astype(BF16)
     ranks = dot(named.astype(BF16), before, 1, 0)
     keys = jnp.where(named > 0.0, ranks, -1.0)
-    for copy in loads:
+    for copy in packing + loads:
         copy.wait()
+    packed_out = pltpu.make_async_copy(packed_buf, packed_ref, weight_sems.at[len(packing)])
+    packed_out.start()
     tokens = tokens_buf[...]
     grads = jnp.concatenate([grads_buf[...], grads_buf[...]], axis=0)
     block = experts // CHUNKS
@@ -131,7 +134,7 @@
             pltpu.make_async_copy(send_buf.at[here], send_ref.at[here], send_sems.at[i])
         )
         sends[i].start()
-    for copy in packing + sends:
+    for copy in [packed_out] + sends:
         copy.wait()
 
 
@@ -165,8 +168,8 @@
         )
 
     fetches = [
-        fetch(0, ins_ref.at[:, :, :hidden_width]),
-        fetch(1, ins_ref.at[:, :, hidden_width:]),
+        fetch(0, ins_ref.at[:, :share, :]),
+        fetch(1, ins_ref.at[:, share:, :]),
         fetch(2, down_ref),
     ]
     block = sources // CHUNKS
@@ -188,8 +191,8 @@
         copy.start()
     fetches[1].wait()
     fetches[2].wait()
-    w_gate = ins_ref[:, :, :hidden_width].reshape(width, hidden_width)
-    w_up = ins_ref[:, :, hidden_width:].reshape(width, hidden_width)
+    w_gate = ins_ref[:, :share, :].reshape(width, hidden_width)
+    w_up = ins_ref[:, share:, :].reshape(width, hidden_width)
     down = jnp.concatenate(
         [
             down_ref[:, :half, :].reshape(hidden_width, hidden_width),
@@ -200,22 +203,21 @@
     count = block * capacity
     tiles = capacity // TILE
     lane = lax.broadcasted_iota(jnp.int32, (block, TILE, PANEL), 2)
-    for i in range(CHUNKS):
+
+    def products(i):
         here = slice(i * block, (i + 1) * block)
-        where = slice(i * count, (i + 1) * count)
-        if i > 0:
-            arrivals[i].wait()
         rows = rows_ref[here, :, :width].reshape(count, width)
         scaled = rows_ref[here, :, width:].reshape(count, width)
-        gate_pre = dot(rows, w_gate, 1, 0)
-        up_proj = dot(rows, w_up, 1, 0)
-        hidden_grad = dot(scaled, down, 1, 1)
+        return dot(rows, w_gate, 1, 0), dot(rows, w_up, 1, 0), dot(scaled, down, 1, 1)
+
+    def activations(i, gate_pre, up_proj, hidden_grad):
+        where = slice(i * count, (i + 1) * count)
         sig = jax.nn.sigmoid(gate_pre)
         act = gate_pre * sig
         hidden = (act * up_proj).astype(BF16)
         hidden_ref[where, :] = hidden
         grads_ref[where, hidden_width:] = (hidden_grad * act).astype(BF16)
-        pre_grad = hidden_grad * up_proj * (sig * (1.0 + gate_pre * (1.0 - sig)))
+        pre_grad = hidden_grad * up_proj * (sig + act * (1.0 - sig))
         grads_ref[where, :hidden_width] = pre_grad.astype(BF16)
         gate_grad = jnp.sum(hidden.astype(F32) * hidden_grad, axis=1, keepdims=True)
         gate_grad = gate_grad.reshape(block, tiles, TILE, 1)
@@ -225,7 +227,15 @@
             high, low = split_high_low(value)
             tile = jnp.where(lane == 2 * n, high.astype(F32), tile)
             tile = jnp.where(lane == 2 * n + 1, low.astype(F32), tile)
-        gate_ref[here] = tile.astype(BF16)
+        gate_ref[i * block : (i + 1) * block] = tile.astype(BF16)
+
+    ahead = products(0)
+    for i in range(CHUNKS):
+        now = ahead
+        if i + 1 < CHUNKS:
+            arrivals[i + 1].wait()
+            ahead = products(i + 1)
+        activations(i, *now)
 
     def store(k):
         return pltpu.make_async_copy(
@@ -248,34 +258,28 @@
         copy.wait()
 
 
-def input_kernel(core_ref, grads_ref, gate_ref, weights_ref, back_ref, ins_ref, sems):
+def input_kernel(core_ref, grads_ref, gate_ref, weights_ref, back_ref, ins_ref, sem):
     sources, panels, _, _ = back_ref.shape
     share = weights_ref.shape[2] // 3
-    pieces, hidden_width = ins_ref.shape[0], ins_ref.shape[2] // 2
+    pieces, _, hidden_width = ins_ref.shape
     core = core_ref[0]
-    span = PANEL // share
-    loads = []
-    for n in range(pieces // span):
-        here = slice(n * span, (n + 1) * span)
-        for k in range(2):
-            loads.append(
-                pltpu.make_async_copy(
-                    weights_ref.at[here, core, k * share : (k + 1) * share, :],
-                    ins_ref.at[here, :, k * hidden_width : (k + 1) * hidden_width],
-                    sems.at[n, k],
-                )
-            )
-    for copy in loads:
-        copy.start()
+    load = pltpu.make_async_copy(weights_ref.at[:, core, : 2 * share, :], ins_ref, sem)
+    load.start()
     back_ref[:, panels - 1] = gate_ref[...]
-    grads = grads_ref[...]
-    tiles = (panels - 1) * span // pieces
-    for n in range(pieces // span):
-        loads[2 * n].wait()
-        loads[2 * n + 1].wait()
-        weights = ins_ref[n * span : (n + 1) * span].reshape(PANEL, 2 * hidden_width)
-        panel = dot(grads, weights, 1, 1).astype(BF16)
-        back_ref[:, n * tiles : (n + 1) * tiles] = panel.reshape(sources, tiles, TILE, PANEL)
+    load.wait()
+    width = pieces * share
+    w_gate = ins_ref[:, :share, :].reshape(width, hidden_width)
+    w_up = ins_ref[:, share:, :].reshape(width, hidden_width)
+    weights = jnp.concatenate([w_gate, w_up], axis=1)
+    block = sources // CHUNKS
+    count = grads_ref.shape[0] // CHUNKS
+    tiles = (panels - 1) * PANEL // width
+    for i in range(CHUNKS):
+        here = slice(i * block, (i + 1) * block)
+        grad = dot(grads_ref[i * count : (i + 1) * count, :], weights, 1, 1).astype(BF16)
+        for n in range(width // PANEL):
+            panel = grad[:, n * PANEL : (n + 1) * PANEL]
+            back_ref[here, n * tiles : (n + 1) * tiles] = panel.reshape(block, tiles, TILE, PANEL)
 
 
 def combine_kernel(members, ids_ref, gates_ref, slots_ref, back_ref, input_ref, gate_ref):
@@ -357,7 +361,8 @@
             pltpu.VMEM((token_count, width), BF16),
             pltpu.VMEM((token_count, width), BF16),
             pltpu.VMEM((experts, capacity, 2 * width), BF16),
-            pltpu.SemaphoreType.DMA((4,)),
+            pltpu.VMEM((members, depth, hidden_width), BF16),
+            pltpu.SemaphoreType.DMA((5,)),
             pltpu.SemaphoreType.DMA((2,)),
             pltpu.SemaphoreType.DMA((CHUNKS,)),
         ],
@@ -393,7 +398,7 @@
             vmem_result(experts, TILE, PANEL),
         ),
         scratch_shapes=[
-            pltpu.VMEM((dp_size, share, 2 * hidden_width), BF16),
+            pltpu.VMEM((dp_size, 2 * share, hidden_width), BF16),
             pltpu.VMEM((experts, capacity, 2 * width), BF16),
             pltpu.VMEM((dp_size, share, hidden_width), BF16),
             pltpu.VMEM((slot_count, hidden_width), BF16),
@@ -421,8 +426,8 @@
         out_specs=vmem,
         out_shape=vmem_result(experts, panels, TILE, PANEL),
         scratch_shapes=[
-            pltpu.VMEM((dp_size, share, 2 * hidden_width), BF16),
-            pltpu.SemaphoreType.DMA((width // PANEL, 2)),
+            pltpu.VMEM((dp_size, 2 * share, hidden_width), BF16),
+            pltpu.SemaphoreType.DMA,
         ],
         compiler_params=params(24),
         name="inputs",

time: 162 us -> 153 us (0.944)
  Pallas kernels: 36.2 us -> 24.4 us
  starting transfers between devices: 1.41 us -> 3.19 us
    pallas_call x1, Pallas kernels: 13.8 us -> 4.8 us  [shards(): pl.pallas_call(functools.partial(dispatch_kernel, members), in_specs=[vme...]
    pallas_call x1, Pallas kernels: 7.28 us -> 4.51 us  [shards(): pl.pallas_call(input_kernel, in_specs=[smem, vmem, vmem, anywhere], out_s...]
    ppermute x1, starting transfers between devices: 1.33 us -> 3.11 us  [shards(): got = lax.ppermute(other, 'dp', [(i, i ^ 1) for i in range(dp_size)])]
  transfers between devices with their start and end apart: 3 -> 3, of which waited for: 0 -> 1; matrix products, arithmetic and copies ran while one was open for 0% -> 0% of each run, Pallas kernels for 5% -> 4%
where the time goes in v5:
time: 153 us; the launch traced here: 152 us
  blocking collectives  109 us (71%)
  Pallas kernels  24.4 us (16%)
  between operations  14.1 us (9%)
  starting transfers between devices  3.19 us (2%)
    all_to_all x2, blocking collectives, exchange(): lax.all_to_all(x, ('dp', 'expert'), split_axis=0, concat_axis=0, tiled=Tr...  109 us
    pallas_call x1, Pallas kernels, shards(): pl.pallas_call(expert_kernel, in_specs=[smem, anywhere, anywhere], out_sp...  12.9 us
    pallas_call x1, Pallas kernels, shards(): pl.pallas_call(functools.partial(dispatch_kernel, members), in_specs=[vme...  4.8 us
    pallas_call x1, Pallas kernels, shards(): pl.pallas_call(input_kernel, in_specs=[smem, vmem, vmem, anywhere], out_s...  4.51 us
    ppermute x1, starting transfers between devices, shards(): got = lax.ppermute(other, 'dp', [(i, i ^ 1) for i in range(dp_size)])  3.11 us
  transfers between devices with their start and end apart: 3, of which 1 were waited for; matrix products, arithmetic and copies ran while one was open for 0% of the time, Pallas kernels for 4%

profile of v5, /device:TPU:1, one launch (start us, length us, event | category | flops | bytes accessed | tf_op | source)
XLA Modules:
  0.0 152.5 jit_solution(10888251412852438540)
XLA Ops:
  7.2 0.0 all-gather.3.cloned.1.call-start
  7.2 4.8 %dispatch.1 = (bf16[32,40,2048]{2,1,0:T(8,128)(2,1)}, bf16[1280,128]{1,0:T(8,128)(2,1)S(1)}, bf16[2,192,512]{2,1,0:T(8,128)(2,1)}) custom-call(s32[8,128]{1,0:T(8,128)} %bitcast.11, f32[8,128]{1,0:T(8,128)} %bitcast.13, bf16[128,1024]{1,0:T(8,128)(2,1)} %tokens_ref.1, bf16[128,1024]{1,0:T(8,128)(2,1)} %grads_ref.1, bf16[2,64,512]{2,1,0:T(8,128)(2,1)} %w_gate_ref.1, ...), custom_call_target="tpu_custom_call" | custom-call | tf_op jit(solution)/shard_map/dispatch/pallas_call | solution.py:351
  12.0 0.0 all-gather.3.cloned.1.call-update
  12.1 0.0 reduce-scatter.2.cloned.1.call-start
  12.1 70.2 %all_to_all.10.recv_ref = bf16[32,40,2048]{2,1,0:T(8,128)(2,1)} all-to-all(bf16[32,40,2048]{2,1,0:T(8,128)(2,1)} %get-tuple-element.24), channel_id=1, replica_groups={{0,1,2,3,4,5,6,7,8,9,10,11,12,13,14,15,16,17,18,19,20,21,22,23,24,25,26..., dimensions={0} | all-to-all | bytes 10485760 | tf_op jit(solution)/shard_map/all_to_all | solution.py:380
  82.3 0.0 all-gather.3.cloned.1.call-done
  82.3 12.9 %expert.1 = (bf16[16,192,512]{2,1,0:T(8,128)(2,1)}, bf16[1280,1024]{1,0:T(8,128)(2,1)S(1)}, bf16[32,8,256]{2,1,0:T(8,128)(2,1)S(1)}) custom-call(s32[1]{0:T(128)} %bitcast.1.core_ref, bf16[32,40,2048]{2,1,0:T(8,128)(2,1)} %all_to_all.10.recv_ref, bf16[16,2,192,512]{3,2,1,0:T(8,128)(2,1)} %bitcast.15), custom_call_target="tpu_custom_call" | custom-call | tf_op jit(solution)/shard_map/expert/pallas_call | solution.py:391
  95.2 0.0 reduce-scatter.2.cloned.1.call-update
  95.2 4.5 %inputs.1 = bf16[32,21,8,256]{3,2,1,0:T(8,128)(2,1)S(1)} custom-call(s32[1]{0:T(128)} %bitcast.1.core_ref, bf16[1280,1024]{1,0:T(8,128)(2,1)S(1)} %get-tuple-element.26.grads_ref, bf16[32,8,256]{2,1,0:T(8,128)(2,1)S(1)} %get-tuple-element.27.gate_ref, bf16[16,2,192,512]{3,2,1,0:T(8,128)(2,1)} %bitcast.16), custom_call_target="tpu_custom_call" | custom-call | tf_op jit(solution)/shard_map/inputs/pallas_call | solution.py:423
  99.7 0.0 copy-start.1
  99.8 0.0 copy-start.2
  99.8 39.0 %all_to_all.11.back_ref = bf16[32,21,8,256]{3,2,1,0:T(8,128)(2,1)S(1)} all-to-all(bf16[32,21,8,256]{3,2,1,0:T(8,128)(2,1)S(1)} %inputs.1), channel_id=1, replica_groups={{0,1,2,3,4,5,6,7,8,9,10,11,12,13,14,15,16,17,18,19,20,21,22,23,24,25,26..., dimensions={0} | all-to-all | bytes 5505024 | tf_op jit(solution)/shard_map/all_to_all | solution.py:380
  138.8 0.4 reduce-scatter.2.cloned.1.call-done
  139.2 0.0 copy-start
  139.2 1.1 select_bitcast_fusion
  140.3 3.1 %collective-permute-start = (bf16[192,512]{1,0:T(8,128)(2,1)S(1)}, bf16[192,512]{1,0:T(8,128)(2,1)S(1)}, u32[]{:S(2)}, u32[]{:S(2)}) collective-permute-start(bf16[192,512]{1,0:T(8,128)(2,1)S(1)} %select_bitcast_fusion), channel_id=1, source_target_pairs={{0,16},{16,0},{32,48},{48,32},{64,80},{80,64},{96,112},{112,96},{1... | collective-permute-start | bytes 589832 | tf_op jit(solution)/shard_map/ppermute | solution.py:437
  143.4 0.0 copy-done.1
  143.4 0.0 copy-done.2
  143.4 1.3 combine.1
  144.7 0.0 collective-permute-done.got_ref
  144.7 0.0 copy-done
  144.7 0.9 scale.1
Async XLA Ops:
  7.2 75.1 %all-gather.3.cloned.1.call-start = ((), (), s32[]{:S(2)}) async-start(), calls=%async_computation.4 | async-start | bytes 6684672 | tf_op jit(solution)/shard_map/all_gather | solution.py:372
  12.1 127.2 %reduce-scatter.2.cloned.1.call-start = ((), (), s32[]{:S(2)}) async-start(), calls=%async_computation.3 | async-start | bytes 3538944 | tf_op jit(solution)/shard_map/reduce_scatter | solution.py:414
  99.7 43.7 %copy-start.1 = (s32[128,8]{0,1:T(8,128)S(1)}, s32[128,8]{0,1:T(8,128)}, u32[]{:S(2)}) copy-start(s32[128,8]{0,1:T(8,128)} %param.9) | copy-start | bytes 12292
  99.8 43.7 %copy-start.2 = (f32[128,8]{0,1:T(8,128)S(1)}, f32[128,8]{0,1:T(8,128)}, u32[]{:S(2)}) copy-start(f32[128,8]{0,1:T(8,128)} %param.10) | copy-start | bytes 12292
  139.2 5.5 %copy-start = (bf16[1,2,192,512]{3,2,1,0:T(8,128)(2,1)S(1)}, bf16[1,2,192,512]{3,2,1,0:T(8,128)(2,1)}, u32[]{:S(2)}) copy-start(bf16[1,2,192,512]{3,2,1,0:T(8,128)(2,1)} %reduce-scatter.2.cloned.1.call-done) | copy-start | bytes 1179652
  140.3 4.4 %collective-permute-start = (bf16[192,512]{1,0:T(8,128)(2,1)S(1)}, bf16[192,512]{1,0:T(8,128)(2,1)S(1)}, u32[]{:S(2)}, u32[]{:S(2)}) collective-permute-start(bf16[192,512]{1,0:T(8,128)(2,1)S(1)} %select_bitcast_fusion), channel_id=1, source_target_pairs={{0,16},{16,0},{32,48},{48,32},{64,80},{80,64},{96,112},{112,96},{1... | collective-permute-start | bytes 589832 | tf_op jit(solution)/shard_map/ppermute | solution.py:437
Sparse Core Ops, SparseCore 0:
  12.2 50.2 all-gather.2
  95.3 43.8 reduce-scatter.1

commit v6 on v5

--- a/solution.py
+++ b/solution.py
@@ -39,12 +39,6 @@
 def split_high_low(x):
     high = x.astype(BF16)
     return high, (x - high.astype(F32)).astype(BF16)
-
-
-def expert_of_row(shape, members):
-    row = lax.broadcasted_iota(jnp.int32, shape, 0)
-    per_member = shape[0] // members
-    return lax.rem(row, per_member) * members + row // per_member
 
 
 def weight_copies(gate_ref, up_ref, down_ref, packed_buf, sems):
@@ -64,7 +58,7 @@
 
 
 def dispatch_kernel(
-    members,
+    experts,
     ids_ref,
     gates_ref,
     tokens_ref,
@@ -92,10 +86,10 @@
     packing = weight_copies(w_gate_ref, w_up_ref, w_down_ref, packed_buf, weight_sems)
     for copy in packing:
         copy.start()
-    experts, capacity, _ = send_buf.shape
+    capacity = send_buf.shape[0] // experts
     token_count, width = tokens_buf.shape
     ids = ids_ref[...]
-    expert = expert_of_row((experts, token_count), members)
+    expert = lax.broadcasted_iota(jnp.int32, (experts, token_count), 0)
     named = jnp.zeros((experts, token_count), F32)
     gates = jnp.zeros((experts, token_count), F32)
     for k in range(ids.shape[0]):
@@ -126,10 +120,9 @@
         high, low = split_high_low(weighted.reshape(count, token_count))
         rows = dot(slots, tokens, 1, 0)
         scaled = dot(jnp.concatenate([high, low], axis=1), grads, 1, 0)
-        shape = (block, capacity, width)
-        here = slice(start, start + block)
-        send_buf[here, :, :width] = rows.astype(BF16).reshape(shape)
-        send_buf[here, :, width:] = scaled.astype(BF16).reshape(shape)
+        here = slice(i * count, (i + 1) * count)
+        send_buf[here, :width] = rows.astype(BF16)
+        send_buf[here, width:] = scaled.astype(BF16)
         sends.append(
             pltpu.make_async_copy(send_buf.at[here], send_ref.at[here], send_sems.at[i])
         )
@@ -154,11 +147,12 @@
     in_sems,
     out_sems,
 ):
-    sources, capacity, _ = rows_ref.shape
+    sources = gate_ref.shape[0]
+    slot_count = rows_ref.shape[0]
+    capacity = slot_count // sources
     pieces, _, depth, hidden_width = weights_ref.shape
     share = depth // 3
     half = share // 2
-    slot_count = sources * capacity
     width = pieces * share
     core = core_ref[0]
 
@@ -173,10 +167,11 @@
         fetch(2, down_ref),
     ]
     block = sources // CHUNKS
+    count = block * capacity
     arrivals = [
         pltpu.make_async_copy(
-            recv_ref.at[i * block : (i + 1) * block],
-            rows_ref.at[i * block : (i + 1) * block],
+            recv_ref.at[i * count : (i + 1) * count],
+            rows_ref.at[i * count : (i + 1) * count],
             row_sems.at[i],
         )
         for i in range(CHUNKS)
@@ -200,14 +195,13 @@
         ],
         axis=1,
     )
-    count = block * capacity
     tiles = capacity // TILE
     lane = lax.broadcasted_iota(jnp.int32, (block, TILE, PANEL), 2)
 
     def products(i):
-        here = slice(i * block, (i + 1) * block)
-        rows = rows_ref[here, :, :width].reshape(count, width)
-        scaled = rows_ref[here, :, width:].reshape(count, width)
+        here = slice(i * count, (i + 1) * count)
+        rows = rows_ref[here, :width]
+        scaled = rows_ref[here, width:]
         return dot(rows, w_gate, 1, 0), dot(rows, w_up, 1, 0), dot(scaled, down, 1, 1)
 
     def activations(i, gate_pre, up_proj, hidden_grad):
@@ -237,24 +231,38 @@
             ahead = products(i + 1)
         activations(i, *now)
 
-    def store(k):
-        return pltpu.make_async_copy(
-            stage_ref.at[k], parts_ref.at[:, k * share : (k + 1) * share, :], out_sems.at[k]
-        )
-
-    stores = [store(k) for k in range(3)]
-    rows = rows_ref[:, :, :width].reshape(slot_count, width)
+    def stores(k):
+        return [
+            pltpu.make_async_copy(
+                stage_ref.at[k, c],
+                parts_ref.at[:, core if c == 0 else 1 - core, k * share : (k + 1) * share, :],
+                out_sems.at[k, c],
+            )
+            for c in range(2)
+        ]
+
+    sent = []
+    rows = rows_ref[:, :width]
     for k in range(2):
         own = grads_ref[:, k * hidden_width : (k + 1) * hidden_width]
         total = dot(rows, own, 0, 0).astype(BF16)
-        stage_ref[k] = total.reshape(pieces, share, hidden_width)
-        stores[k].start()
-    scaled = rows_ref[:, :, width:].reshape(slot_count, width)
+        total = total.reshape(pieces // 2, 2, share, hidden_width)
+        for c in range(2):
+            stage_ref[k, c] = total[:, c]
+        sent += stores(k)
+        for copy in sent[-2:]:
+            copy.start()
+    scaled = rows_ref[:, width:]
     total = dot(hidden_ref[...], scaled, 0, 0).astype(BF16)
-    stage_ref[2, :, :half, :] = total[:, :hidden_width].reshape(pieces, half, hidden_width)
-    stage_ref[2, :, half:, :] = total[:, hidden_width:].reshape(pieces, half, hidden_width)
-    stores[2].start()
-    for copy in stores:
+    for n in range(2):
+        side = total[:, n * hidden_width : (n + 1) * hidden_width]
+        side = side.reshape(pieces // 2, 2, half, hidden_width)
+        for c in range(2):
+            stage_ref[2, c, :, n * half : (n + 1) * half, :] = side[:, c]
+    sent += stores(2)
+    for copy in sent[-2:]:
+        copy.start()
+    for copy in sent:
         copy.wait()
 
 
@@ -282,7 +290,7 @@
             back_ref[here, n * tiles : (n + 1) * tiles] = panel.reshape(block, tiles, TILE, PANEL)
 
 
-def combine_kernel(members, ids_ref, gates_ref, slots_ref, back_ref, input_ref, gate_ref):
+def combine_kernel(ids_ref, gates_ref, slots_ref, back_ref, input_ref, gate_ref):
     experts, panels, _, _ = back_ref.shape
     top, token_count = ids_ref.shape
     width = input_ref.shape[1]
@@ -299,7 +307,7 @@
         value = extra[:, :, 2 * n : 2 * n + 1] + extra[:, :, 2 * n + 1 : 2 * n + 2]
         picked = jnp.where(hits[:, n * TILE : (n + 1) * TILE, :] > 0.0, value, 0.0)
         by_expert = by_expert + jnp.sum(picked, axis=1)
-    expert = expert_of_row((experts, token_count), members)
+    expert = lax.broadcasted_iota(jnp.int32, (experts, token_count), 0)
     ids = ids_ref[...]
     for k in range(top):
         own = jnp.where(ids[k : k + 1, :] == expert, by_expert, 0.0)
@@ -313,18 +321,15 @@
     core = core_ref[0]
 
     def put(member, value):
-        value = value.astype(F32) * scale
-        gate_ref[member] = value[:share]
-        up_ref[member] = value[share : 2 * share]
-        down_ref[member, :, :hidden_width] = value[2 * share : 2 * share + half]
-        down_ref[member, :, hidden_width:] = value[2 * share + half :]
-
-    for c in range(2):
-
-        @pl.when(core == c)
-        def _(c=c):
-            put(c, sums_ref[c])
-            put(1 - c, got_ref[...])
+        value = (value.astype(F32) * scale)[None]
+        here = pl.ds(member, 1)
+        gate_ref[here] = value[:, :share]
+        up_ref[here] = value[:, share : 2 * share]
+        down_ref[here, :, :hidden_width] = value[:, 2 * share : 2 * share + half]
+        down_ref[here, :, hidden_width:] = value[:, 2 * share + half :]
+
+    put(core, sums_ref[0])
+    put(1 - core, got_ref[...])
 
 
 def shards(tokens, out_grad, route_ids, route_gates, w_gate, w_up, w_down):
@@ -345,22 +350,21 @@
     anywhere = pl.BlockSpec(memory_space=pl.ANY)
 
     core = lax.rem(lax.axis_index("dp"), members).astype(jnp.int32).reshape(1)
-    first = core[0] == 0
-    ids, core, first = lax.optimization_barrier((route_ids.T, core, first))
+    ids, core = lax.optimization_barrier((route_ids.T, core))
     gates = route_gates.T
     send, slots, packed = pl.pallas_call(
-        functools.partial(dispatch_kernel, members),
+        functools.partial(dispatch_kernel, experts),
         in_specs=[vmem, vmem] + [anywhere] * 5,
         out_specs=(anywhere, vmem, anywhere),
         out_shape=(
-            hbm_result(experts, capacity, 2 * width),
+            hbm_result(slot_count, 2 * width),
             vmem_result(slot_count, token_count),
             hbm_result(members, depth, hidden_width),
         ),
         scratch_shapes=[
             pltpu.VMEM((token_count, width), BF16),
             pltpu.VMEM((token_count, width), BF16),
-            pltpu.VMEM((experts, capacity, 2 * width), BF16),
+            pltpu.VMEM((slot_count, 2 * width), BF16),
             pltpu.VMEM((members, depth, hidden_width), BF16),
             pltpu.SemaphoreType.DMA((5,)),
             pltpu.SemaphoreType.DMA((2,)),
@@ -372,7 +376,7 @@
     weights = lax.all_gather(packed, "dp", axis=0, tiled=False)
 
     chip_plane = [
-        [(chip * members + c) * expert_size + e for c in range(members) for e in range(expert_size)]
+        [(chip * members + c) * expert_size + e for e in range(expert_size) for c in range(members)]
         for chip in range(chips)
     ]
 
@@ -386,33 +390,33 @@
             axis_index_groups=chip_plane,
         )
 
-    recv = exchange(send)
+    recv = exchange(send.reshape(experts, capacity, 2 * width)).reshape(slot_count, 2 * width)
 
     parts, row_grads, gate_tiles = pl.pallas_call(
         expert_kernel,
         in_specs=[smem, anywhere, anywhere],
         out_specs=(anywhere, vmem, vmem),
         out_shape=(
-            hbm_result(dp_size, depth, hidden_width),
+            hbm_result(chips, members, depth, hidden_width),
             vmem_result(slot_count, 2 * hidden_width),
             vmem_result(experts, TILE, PANEL),
         ),
         scratch_shapes=[
             pltpu.VMEM((dp_size, 2 * share, hidden_width), BF16),
-            pltpu.VMEM((experts, capacity, 2 * width), BF16),
+            pltpu.VMEM((slot_count, 2 * width), BF16),
             pltpu.VMEM((dp_size, share, hidden_width), BF16),
             pltpu.VMEM((slot_count, hidden_width), BF16),
-            pltpu.VMEM((3, dp_size, share, hidden_width), BF16),
+            pltpu.VMEM((3, members, chips, share, hidden_width), BF16),
             pltpu.SemaphoreType.DMA((CHUNKS,)),
             pltpu.SemaphoreType.DMA((3,)),
-            pltpu.SemaphoreType.DMA((3,)),
+            pltpu.SemaphoreType.DMA((3, members)),
         ],
         compiler_params=params(40),
         name="expert",
     )(core, in_hbm(recv), in_hbm(weights))
     same_core = [list(range(c, dp_size, members)) for c in range(members)]
     sums = lax.psum_scatter(
-        parts.reshape(chips, members, depth, hidden_width),
+        parts,
         "dp",
         scatter_dimension=0,
         tiled=False,
@@ -433,10 +437,9 @@
         name="inputs",
     )(core, in_vmem(row_grads), in_vmem(gate_tiles), in_hbm(weights))
     back, sums = lax.optimization_barrier((exchange(back), sums))
-    other = jnp.where(first, sums[1], sums[0])
-    got = lax.ppermute(other, "dp", [(i, i ^ 1) for i in range(dp_size)])
+    got = lax.ppermute(sums[1], "dp", [(i, i ^ 1) for i in range(dp_size)])
     input_grad, gate_grad = pl.pallas_call(
-        functools.partial(combine_kernel, members),
+        combine_kernel,
         out_shape=(
             jax.ShapeDtypeStruct((token_count, width), BF16),
             jax.ShapeDtypeStruct((top, token_count), F32),

time: 153 us -> 154 us (level)
  blocking collectives: 109 us -> 111 us
  transfers between devices with their start and end apart: 3 -> 3, of which waited for: 1 -> 0; matrix products, arithmetic and copies ran while one was open for 0% -> 0% of each run, Pallas kernels for 4% -> 4%
where the time goes in v6:
time: 154 us; the launch traced here: 153 us
  blocking collectives  111 us (72%)
  Pallas kernels  24.4 us (16%)
  between operations  14.1 us (9%)
  starting transfers between devices  3.25 us (2%)
    all_to_all x2, blocking collectives, exchange(): lax.all_to_all(x, ('dp', 'expert'), split_axis=0, concat_axis=0, tiled=Tr...  111 us
    pallas_call x1, Pallas kernels, shards(): pl.pallas_call(expert_kernel, in_specs=[smem, anywhere, anywhere], out_sp...  12.9 us
    pallas_call x1, Pallas kernels, shards(): pl.pallas_call(functools.partial(dispatch_kernel, experts), in_specs=[vme...  4.8 us
    pallas_call x1, Pallas kernels, shards(): pl.pallas_call(input_kernel, in_specs=[smem, vmem, vmem, anywhere], out_s...  4.51 us
    ppermute x1, starting transfers between devices, shards(): got = lax.ppermute(sums[1], 'dp', [(i, i ^ 1) for i in range(dp_size)])  3.17 us
  transfers between devices with their start and end apart: 3, of which 0 were waited for; matrix products, arithmetic and copies ran while one was open for 0% of the time, Pallas kernels for 4%

profile of v6, /device:TPU:1, one launch (start us, length us, event | category | flops | bytes accessed | tf_op | source)
XLA Modules:
  0.0 153.4 jit_solution(7025007726983573574)
XLA Ops:
  7.2 0.0 all-gather.3.cloned.1.call-start
  7.2 4.8 %dispatch.1 = (bf16[1280,2048]{1,0:T(8,128)(2,1)}, bf16[1280,128]{1,0:T(8,128)(2,1)S(1)}, bf16[2,192,512]{2,1,0:T(8,128)(2,1)}) custom-call(s32[8,128]{1,0:T(8,128)} %bitcast.12, f32[8,128]{1,0:T(8,128)} %bitcast.14, bf16[128,1024]{1,0:T(8,128)(2,1)} %tokens_ref.1, bf16[128,1024]{1,0:T(8,128)(2,1)} %grads_ref.1, bf16[2,64,512]{2,1,0:T(8,128)(2,1)} %w_gate_ref.1, ...), custom_call_target="tpu_custom_call" | custom-call | tf_op jit(solution)/shard_map/dispatch/pallas_call | solution.py:355
  12.0 0.0 all-gather.3.cloned.1.call-update
  12.1 0.0 reduce-scatter.2.cloned.1.call-start
  12.1 70.8 %all_to_all.10 = bf16[32,40,2048]{2,1,0:T(8,128)(2,1)} all-to-all(bf16[32,40,2048]{2,1,0:T(8,128)(2,1)} %bitcast.19), channel_id=1, replica_groups={{0,16,1,17,2,18,3,19,4,20,5,21,6,22,7,23,8,24,9,25,10,26,11,27,12,28,13..., dimensions={0} | all-to-all | bytes 10485760 | tf_op jit(solution)/shard_map/all_to_all | solution.py:384
  82.9 0.0 all-gather.3.cloned.1.call-done
  82.9 12.9 %expert.1 = (bf16[8,2,192,512]{3,2,1,0:T(8,128)(2,1)}, bf16[1280,1024]{1,0:T(8,128)(2,1)S(1)}, bf16[32,8,256]{2,1,0:T(8,128)(2,1)S(1)}) custom-call(s32[1]{0:T(128)} %bitcast.1.core_ref, bf16[1280,2048]{1,0:T(8,128)(2,1)} %bitcast.18, bf16[16,2,192,512]{3,2,1,0:T(8,128)(2,1)} %bitcast.16), custom_call_target="tpu_custom_call" | custom-call | tf_op jit(solution)/shard_map/expert/pallas_call | solution.py:395
  95.9 0.0 reduce-scatter.2.cloned.1.call-update
  95.9 4.5 %inputs.1 = bf16[32,21,8,256]{3,2,1,0:T(8,128)(2,1)S(1)} custom-call(s32[1]{0:T(128)} %bitcast.1.core_ref, bf16[1280,1024]{1,0:T(8,128)(2,1)S(1)} %get-tuple-element.25.grads_ref, bf16[32,8,256]{2,1,0:T(8,128)(2,1)S(1)} %get-tuple-element.26.gate_ref, bf16[16,2,192,512]{3,2,1,0:T(8,128)(2,1)} %bitcast.17), custom_call_target="tpu_custom_call" | custom-call | tf_op jit(solution)/shard_map/inputs/pallas_call | solution.py:427
  100.4 0.0 copy-start.1
  100.4 0.0 copy-start.2
  100.4 39.7 %all_to_all.11.back_ref = bf16[32,21,8,256]{3,2,1,0:T(8,128)(2,1)S(1)} all-to-all(bf16[32,21,8,256]{3,2,1,0:T(8,128)(2,1)S(1)} %inputs.1), channel_id=1, replica_groups={{0,16,1,17,2,18,3,19,4,20,5,21,6,22,7,23,8,24,9,25,10,26,11,27,12,28,13..., dimensions={0} | all-to-all | bytes 5505024 | tf_op jit(solution)/shard_map/all_to_all | solution.py:384
  140.1 0.0 reduce-scatter.2.cloned.1.call-done
  140.1 0.0 copy-start
  140.1 1.0 slice_bitcast_fusion
  141.1 3.2 %collective-permute-start = (bf16[192,512]{1,0:T(8,128)(2,1)S(1)}, bf16[192,512]{1,0:T(8,128)(2,1)S(1)}, u32[]{:S(2)}, u32[]{:S(2)}) collective-permute-start(bf16[192,512]{1,0:T(8,128)(2,1)S(1)} %slice_bitcast_fusion), channel_id=1, source_target_pairs={{0,16},{16,0},{32,48},{48,32},{64,80},{80,64},{96,112},{112,96},{1... | collective-permute-start | bytes 589832 | tf_op jit(solution)/shard_map/ppermute | solution.py:440
  144.3 0.0 copy-done.1
  144.3 0.0 copy-done.2
  144.3 1.3 combine.1
  145.6 0.0 collective-permute-done.got_ref
  145.6 0.0 copy-done
  145.6 0.9 scale.1
Async XLA Ops:
  7.2 75.8 %all-gather.3.cloned.1.call-start = ((), (), s32[]{:S(2)}) async-start(), calls=%async_computation.4 | async-start | bytes 6684672 | tf_op jit(solution)/shard_map/all_gather | solution.py:376
  12.1 128.1 %reduce-scatter.2.cloned.1.call-start = ((), (), s32[]{:S(2)}) async-start(), calls=%async_computation.3 | async-start | bytes 3538944 | tf_op jit(solution)/shard_map/reduce_scatter | solution.py:418
  100.4 43.9 %copy-start.1 = (s32[128,8]{0,1:T(8,128)S(1)}, s32[128,8]{0,1:T(8,128)}, u32[]{:S(2)}) copy-start(s32[128,8]{0,1:T(8,128)} %param.9) | copy-start | bytes 12292
  100.4 43.9 %copy-start.2 = (f32[128,8]{0,1:T(8,128)S(1)}, f32[128,8]{0,1:T(8,128)}, u32[]{:S(2)}) copy-start(f32[128,8]{0,1:T(8,128)} %param.10) | copy-start | bytes 12292
  140.1 5.5 %copy-start = (bf16[1,2,192,512]{3,2,1,0:T(8,128)(2,1)S(1)}, bf16[1,2,192,512]{3,2,1,0:T(8,128)(2,1)}, u32[]{:S(2)}) copy-start(bf16[1,2,192,512]{3,2,1,0:T(8,128)(2,1)} %reduce-scatter.2.cloned.1.call-done) | copy-start | bytes 1179652
  141.1 4.5 %collective-permute-start = (bf16[192,512]{1,0:T(8,128)(2,1)S(1)}, bf16[192,512]{1,0:T(8,128)(2,1)S(1)}, u32[]{:S(2)}, u32[]{:S(2)}) collective-permute-start(bf16[192,512]{1,0:T(8,128)(2,1)S(1)} %slice_bitcast_fusion), channel_id=1, source_target_pairs={{0,16},{16,0},{32,48},{48,32},{64,80},{80,64},{96,112},{112,96},{1... | collective-permute-start | bytes 589832 | tf_op jit(solution)/shard_map/ppermute | solution.py:440
Sparse Core Ops, SparseCore 0:
  12.2 50.2 all-gather.2
  96.0 43.9 reduce-scatter.1

commit v7 on v6

--- a/solution.py
+++ b/solution.py
@@ -14,6 +14,7 @@
 TILE = 8
 PANEL = 256
 CHUNKS = 4
+SEND_CHUNKS = 8
 
 
 def in_vmem(x):
@@ -107,11 +108,11 @@
     packed_out.start()
     tokens = tokens_buf[...]
     grads = jnp.concatenate([grads_buf[...], grads_buf[...]], axis=0)
-    block = experts // CHUNKS
+    block = experts // SEND_CHUNKS
     count = block * capacity
     place = lax.broadcasted_iota(jnp.int32, (block, capacity, token_count), 1).astype(F32)
     sends = []
-    for i in range(CHUNKS):
+    for i in range(SEND_CHUNKS):
         start = i * block
         hit = keys[start : start + block, None, :] == place
         slots = jnp.where(hit, 1.0, 0.0).reshape(count, token_count).astype(BF16)
@@ -329,7 +330,7 @@
         down_ref[here, :, hidden_width:] = value[:, 2 * share + half :]
 
     put(core, sums_ref[0])
-    put(1 - core, got_ref[...])
+    put(1 - core, got_ref[1])
 
 
 def shards(tokens, out_grad, route_ids, route_gates, w_gate, w_up, w_down):
@@ -368,7 +369,7 @@
             pltpu.VMEM((members, depth, hidden_width), BF16),
             pltpu.SemaphoreType.DMA((5,)),
             pltpu.SemaphoreType.DMA((2,)),
-            pltpu.SemaphoreType.DMA((CHUNKS,)),
+            pltpu.SemaphoreType.DMA((SEND_CHUNKS,)),
         ],
         compiler_params=params(24),
         name="dispatch",
@@ -437,7 +438,7 @@
         name="inputs",
     )(core, in_vmem(row_grads), in_vmem(gate_tiles), in_hbm(weights))
     back, sums = lax.optimization_barrier((exchange(back), sums))
-    got = lax.ppermute(sums[1], "dp", [(i, i ^ 1) for i in range(dp_size)])
+    got = lax.ppermute(sums, "dp", [(i, i ^ 1) for i in range(dp_size)])
     input_grad, gate_grad = pl.pallas_call(
         combine_kernel,
         out_shape=(

time: 154 us -> 153 us (level)
  transfers between devices with their start and end apart: 3 -> 3, of which waited for: 0 -> 1; matrix products, arithmetic and copies ran while one was open for 0% -> 0% of each run, Pallas kernels for 4% -> 4%
where the time goes in v7:
time: 153 us; the launch traced here: 152 us
  blocking collectives  111 us (73%)
  Pallas kernels  24.3 us (16%)
  between operations  14.1 us (9%)
  starting transfers between devices  3.09 us (2%)
    all_to_all x2, blocking collectives, exchange(): lax.all_to_all(x, ('dp', 'expert'), split_axis=0, concat_axis=0, tiled=Tr...  111 us
    pallas_call x1, Pallas kernels, shards(): pl.pallas_call(expert_kernel, in_specs=[smem, anywhere, anywhere], out_sp...  12.9 us
    pallas_call x1, Pallas kernels, shards(): pl.pallas_call(functools.partial(dispatch_kernel, experts), in_specs=[vme...  4.67 us
    pallas_call x1, Pallas kernels, shards(): pl.pallas_call(input_kernel, in_specs=[smem, vmem, vmem, anywhere], out_s...  4.51 us
  transfers between devices with their start and end apart: 3, of which 1 were waited for; matrix products, arithmetic and copies ran while one was open for 0% of the time, Pallas kernels for 4%

profile of v7, /device:TPU:1, one launch (start us, length us, event | category | flops | bytes accessed | tf_op | source)
XLA Modules:
  0.0 152.4 jit_solution(6699308255308111412)
XLA Ops:
  7.2 0.0 all-gather.3.cloned.1.call-start
  7.2 4.7 %dispatch.1 = (bf16[1280,2048]{1,0:T(8,128)(2,1)}, bf16[1280,128]{1,0:T(8,128)(2,1)S(1)}, bf16[2,192,512]{2,1,0:T(8,128)(2,1)}) custom-call(s32[8,128]{1,0:T(8,128)} %bitcast.10, f32[8,128]{1,0:T(8,128)} %bitcast.12, bf16[128,1024]{1,0:T(8,128)(2,1)} %tokens_ref.1, bf16[128,1024]{1,0:T(8,128)(2,1)} %grads_ref.1, bf16[2,64,512]{2,1,0:T(8,128)(2,1)} %w_gate_ref.1, ...), custom_call_target="tpu_custom_call" | custom-call | tf_op jit(solution)/shard_map/dispatch/pallas_call | solution.py:356
  11.9 0.0 all-gather.3.cloned.1.call-update
  11.9 0.0 reduce-scatter.2.cloned.1.call-start
  12.0 70.8 %all_to_all.10 = bf16[32,40,2048]{2,1,0:T(8,128)(2,1)} all-to-all(bf16[32,40,2048]{2,1,0:T(8,128)(2,1)} %bitcast.17), channel_id=1, replica_groups={{0,16,1,17,2,18,3,19,4,20,5,21,6,22,7,23,8,24,9,25,10,26,11,27,12,28,13..., dimensions={0} | all-to-all | bytes 10485760 | tf_op jit(solution)/shard_map/all_to_all | solution.py:385
  82.8 0.0 all-gather.3.cloned.1.call-done
  82.8 12.9 %expert.1 = (bf16[8,2,192,512]{3,2,1,0:T(8,128)(2,1)}, bf16[1280,1024]{1,0:T(8,128)(2,1)S(1)}, bf16[32,8,256]{2,1,0:T(8,128)(2,1)S(1)}) custom-call(s32[1]{0:T(128)} %bitcast.1.core_ref, bf16[1280,2048]{1,0:T(8,128)(2,1)} %bitcast.16, bf16[16,2,192,512]{3,2,1,0:T(8,128)(2,1)} %bitcast.14), custom_call_target="tpu_custom_call" | custom-call | tf_op jit(solution)/shard_map/expert/pallas_call | solution.py:396
  95.7 0.0 reduce-scatter.2.cloned.1.call-update
  95.8 4.5 %inputs.1 = bf16[32,21,8,256]{3,2,1,0:T(8,128)(2,1)S(1)} custom-call(s32[1]{0:T(128)} %bitcast.1.core_ref, bf16[1280,1024]{1,0:T(8,128)(2,1)S(1)} %get-tuple-element.25.grads_ref, bf16[32,8,256]{2,1,0:T(8,128)(2,1)S(1)} %get-tuple-element.26.gate_ref, bf16[16,2,192,512]{3,2,1,0:T(8,128)(2,1)} %bitcast.15), custom_call_target="tpu_custom_call" | custom-call | tf_op jit(solution)/shard_map/inputs/pallas_call | solution.py:428
  100.3 0.0 copy-start.1
  100.3 0.0 copy-start.2
  100.3 39.7 %all_to_all.11.back_ref = bf16[32,21,8,256]{3,2,1,0:T(8,128)(2,1)S(1)} all-to-all(bf16[32,21,8,256]{3,2,1,0:T(8,128)(2,1)S(1)} %inputs.1), channel_id=1, replica_groups={{0,16,1,17,2,18,3,19,4,20,5,21,6,22,7,23,8,24,9,25,10,26,11,27,12,28,13..., dimensions={0} | all-to-all | bytes 5505024 | tf_op jit(solution)/shard_map/all_to_all | solution.py:385
  140.0 0.0 reduce-scatter.2.cloned.1.call-done
  140.0 0.0 copy-start
  140.0 3.0 %collective-permute-start = (bf16[2,192,512]{2,1,0:T(8,128)(2,1)}, bf16[2,192,512]{2,1,0:T(8,128)(2,1)S(1)}, u32[]{:S(2)}, u32[]{:S(2)}) collective-permute-start(bf16[2,192,512]{2,1,0:T(8,128)(2,1)} %bitcast.8), channel_id=1, source_target_pairs={{0,16},{16,0},{32,48},{48,32},{64,80},{80,64},{96,112},{112,96},{1... | collective-permute-start | bytes 1179656 | tf_op jit(solution)/shard_map/ppermute | solution.py:441
  143.1 0.0 copy-done.1
  143.1 0.0 copy-done.2
  143.1 1.3 combine.1
  144.3 0.3 collective-permute-done.got_ref
  144.6 0.0 copy-done
  144.6 0.9 scale.1
Async XLA Ops:
  7.2 75.6 %all-gather.3.cloned.1.call-start = ((), (), s32[]{:S(2)}) async-start(), calls=%async_computation.4 | async-start | bytes 6684672 | tf_op jit(solution)/shard_map/all_gather | solution.py:377
  11.9 128.1 %reduce-scatter.2.cloned.1.call-start = ((), (), s32[]{:S(2)}) async-start(), calls=%async_computation.3 | async-start | bytes 3538944 | tf_op jit(solution)/shard_map/reduce_scatter | solution.py:419
  100.3 42.8 %copy-start.1 = (s32[128,8]{0,1:T(8,128)S(1)}, s32[128,8]{0,1:T(8,128)}, u32[]{:S(2)}) copy-start(s32[128,8]{0,1:T(8,128)} %param.9) | copy-start | bytes 12292
  100.3 42.8 %copy-start.2 = (f32[128,8]{0,1:T(8,128)S(1)}, f32[128,8]{0,1:T(8,128)}, u32[]{:S(2)}) copy-start(f32[128,8]{0,1:T(8,128)} %param.10) | copy-start | bytes 12292
  140.0 4.6 %copy-start = (bf16[1,2,192,512]{3,2,1,0:T(8,128)(2,1)S(1)}, bf16[1,2,192,512]{3,2,1,0:T(8,128)(2,1)}, u32[]{:S(2)}) copy-start(bf16[1,2,192,512]{3,2,1,0:T(8,128)(2,1)} %reduce-scatter.2.cloned.1.call-done) | copy-start | bytes 1179652
  140.0 4.6 %collective-permute-start = (bf16[2,192,512]{2,1,0:T(8,128)(2,1)}, bf16[2,192,512]{2,1,0:T(8,128)(2,1)S(1)}, u32[]{:S(2)}, u32[]{:S(2)}) collective-permute-start(bf16[2,192,512]{2,1,0:T(8,128)(2,1)} %bitcast.8), channel_id=1, source_target_pairs={{0,16},{16,0},{32,48},{48,32},{64,80},{80,64},{96,112},{112,96},{1... | collective-permute-start | bytes 1179656 | tf_op jit(solution)/shard_map/ppermute | solution.py:441
Sparse Core Ops, SparseCore 0:
  12.0 50.2 all-gather.2
  95.9 44.0 reduce-scatter.1

commit v8 on v7

--- a/solution.py
+++ b/solution.py
@@ -40,6 +40,12 @@
 def split_high_low(x):
     high = x.astype(BF16)
     return high, (x - high.astype(F32)).astype(BF16)
+
+
+def expert_of_row(shape, members):
+    row = lax.broadcasted_iota(jnp.int32, shape, 0)
+    per_member = shape[0] // members
+    return lax.rem(row, per_member) * members + row // per_member
 
 
 def weight_copies(gate_ref, up_ref, down_ref, packed_buf, sems):
@@ -59,6 +65,7 @@
 
 
 def dispatch_kernel(
+    members,
     experts,
     ids_ref,
     gates_ref,
@@ -90,7 +97,7 @@
     capacity = send_buf.shape[0] // experts
     token_count, width = tokens_buf.shape
     ids = ids_ref[...]
-    expert = lax.broadcasted_iota(jnp.int32, (experts, token_count), 0)
+    expert = expert_of_row((experts, token_count), members)
     named = jnp.zeros((experts, token_count), F32)
     gates = jnp.zeros((experts, token_count), F32)
     for k in range(ids.shape[0]):
@@ -291,7 +298,7 @@
             back_ref[here, n * tiles : (n + 1) * tiles] = panel.reshape(block, tiles, TILE, PANEL)
 
 
-def combine_kernel(ids_ref, gates_ref, slots_ref, back_ref, input_ref, gate_ref):
+def combine_kernel(members, ids_ref, gates_ref, slots_ref, back_ref, input_ref, gate_ref):
     experts, panels, _, _ = back_ref.shape
     top, token_count = ids_ref.shape
     width = input_ref.shape[1]
@@ -308,7 +315,7 @@
         value = extra[:, :, 2 * n : 2 * n + 1] + extra[:, :, 2 * n + 1 : 2 * n + 2]
         picked = jnp.where(hits[:, n * TILE : (n + 1) * TILE, :] > 0.0, value, 0.0)
         by_expert = by_expert + jnp.sum(picked, axis=1)
-    expert = lax.broadcasted_iota(jnp.int32, (experts, token_count), 0)
+    expert = expert_of_row((experts, token_count), members)
     ids = ids_ref[...]
     for k in range(top):
         own = jnp.where(ids[k : k + 1, :] == expert, by_expert, 0.0)
@@ -354,7 +361,7 @@
     ids, core = lax.optimization_barrier((route_ids.T, core))
     gates = route_gates.T
     send, slots, packed = pl.pallas_call(
-        functools.partial(dispatch_kernel, experts),
+        functools.partial(dispatch_kernel, members, experts),
         in_specs=[vmem, vmem] + [anywhere] * 5,
         out_specs=(anywhere, vmem, anywhere),
         out_shape=(
@@ -377,7 +384,7 @@
     weights = lax.all_gather(packed, "dp", axis=0, tiled=False)
 
     chip_plane = [
-        [(chip * members + c) * expert_size + e for e in range(expert_size) for c in range(members)]
+        [(chip * members + c) * expert_size + e for c in range(members) for e in range(expert_size)]
         for chip in range(chips)
     ]
 
@@ -440,7 +447,7 @@
     back, sums = lax.optimization_barrier((exchange(back), sums))
     got = lax.ppermute(sums, "dp", [(i, i ^ 1) for i in range(dp_size)])
     input_grad, gate_grad = pl.pallas_call(
-        combine_kernel,
+        functools.partial(combine_kernel, members),
         out_shape=(
             jax.ShapeDtypeStruct((token_count, width), BF16),
             jax.ShapeDtypeStruct((top, token_count), F32),

time: 153 us -> 152 us (level)
  blocking collectives: 111 us -> 109 us
  transfers between devices with their start and end apart: 3 -> 3, of which waited for: 1 -> 2; matrix products, arithmetic and copies ran while one was open for 0% -> 0% of each run, Pallas kernels for 4% -> 4%
where the time goes in v8:
time: 152 us
  blocking collectives  109 us (72%)
  Pallas kernels  24.3 us (16%)
  between operations  14.1 us (9%)
  starting transfers between devices  3.19 us (2%)
    all_to_all x2, blocking collectives, exchange(): lax.all_to_all(x, ('dp', 'expert'), split_axis=0, concat_axis=0, tiled=Tr...  109 us
    pallas_call x1, Pallas kernels, shards(): pl.pallas_call(expert_kernel, in_specs=[smem, anywhere, anywhere], out_sp...  12.9 us
    pallas_call x1, Pallas kernels, shards(): pl.pallas_call(functools.partial(dispatch_kernel, members, experts), in_s...  4.67 us
    pallas_call x1, Pallas kernels, shards(): pl.pallas_call(input_kernel, in_specs=[smem, vmem, vmem, anywhere], out_s...  4.51 us
    ppermute x1, starting transfers between devices, shards(): got = lax.ppermute(sums, 'dp', [(i, i ^ 1) for i in range(dp_size)])  3.11 us
  transfers between devices with their start and end apart: 3, of which 2 were waited for; matrix products, arithmetic and copies ran while one was open for 0% of the time, Pallas kernels for 4%

profile of v8, /device:TPU:1, one launch (start us, length us, event | category | flops | bytes accessed | tf_op | source)
XLA Modules:
  0.0 151.6 jit_solution(5548871212978409561)
XLA Ops:
  7.2 0.0 all-gather.3.cloned.1.call-start
  7.2 4.7 %dispatch.1 = (bf16[1280,2048]{1,0:T(8,128)(2,1)}, bf16[1280,128]{1,0:T(8,128)(2,1)S(1)}, bf16[2,192,512]{2,1,0:T(8,128)(2,1)}) custom-call(s32[8,128]{1,0:T(8,128)} %bitcast.10, f32[8,128]{1,0:T(8,128)} %bitcast.12, bf16[128,1024]{1,0:T(8,128)(2,1)} %tokens_ref.1, bf16[128,1024]{1,0:T(8,128)(2,1)} %grads_ref.1, bf16[2,64,512]{2,1,0:T(8,128)(2,1)} %w_gate_ref.1, ...), custom_call_target="tpu_custom_call" | custom-call | tf_op jit(solution)/shard_map/dispatch/pallas_call | solution.py:363
  11.9 0.0 all-gather.3.cloned.1.call-update
  11.9 0.0 reduce-scatter.2.cloned.1.call-start
  12.0 70.2 %all_to_all.10 = bf16[32,40,2048]{2,1,0:T(8,128)(2,1)} all-to-all(bf16[32,40,2048]{2,1,0:T(8,128)(2,1)} %bitcast.17), channel_id=1, replica_groups={{0,1,2,3,4,5,6,7,8,9,10,11,12,13,14,15,16,17,18,19,20,21,22,23,24,25,26..., dimensions={0} | all-to-all | bytes 10485760 | tf_op jit(solution)/shard_map/all_to_all | solution.py:392
  82.2 0.0 all-gather.3.cloned.1.call-done
  82.2 12.9 %expert.1 = (bf16[8,2,192,512]{3,2,1,0:T(8,128)(2,1)}, bf16[1280,1024]{1,0:T(8,128)(2,1)S(1)}, bf16[32,8,256]{2,1,0:T(8,128)(2,1)S(1)}) custom-call(s32[1]{0:T(128)} %bitcast.1.core_ref, bf16[1280,2048]{1,0:T(8,128)(2,1)} %bitcast.16, bf16[16,2,192,512]{3,2,1,0:T(8,128)(2,1)} %bitcast.14), custom_call_target="tpu_custom_call" | custom-call | tf_op jit(solution)/shard_map/expert/pallas_call | solution.py:403
  95.1 0.0 reduce-scatter.2.cloned.1.call-update
  95.1 4.5 %inputs.1 = bf16[32,21,8,256]{3,2,1,0:T(8,128)(2,1)S(1)} custom-call(s32[1]{0:T(128)} %bitcast.1.core_ref, bf16[1280,1024]{1,0:T(8,128)(2,1)S(1)} %get-tuple-element.25.grads_ref, bf16[32,8,256]{2,1,0:T(8,128)(2,1)S(1)} %get-tuple-element.26.gate_ref, bf16[16,2,192,512]{3,2,1,0:T(8,128)(2,1)} %bitcast.15), custom_call_target="tpu_custom_call" | custom-call | tf_op jit(solution)/shard_map/inputs/pallas_call | solution.py:435
  99.6 0.0 copy-start.1
  99.6 0.0 copy-start.2
  99.7 39.0 %all_to_all.11.back_ref = bf16[32,21,8,256]{3,2,1,0:T(8,128)(2,1)S(1)} all-to-all(bf16[32,21,8,256]{3,2,1,0:T(8,128)(2,1)S(1)} %inputs.1), channel_id=1, replica_groups={{0,1,2,3,4,5,6,7,8,9,10,11,12,13,14,15,16,17,18,19,20,21,22,23,24,25,26..., dimensions={0} | all-to-all | bytes 5505024 | tf_op jit(solution)/shard_map/all_to_all | solution.py:392
  138.7 0.5 reduce-scatter.2.cloned.1.call-done
  139.1 0.0 copy-start
  139.1 3.1 %collective-permute-start = (bf16[2,192,512]{2,1,0:T(8,128)(2,1)}, bf16[2,192,512]{2,1,0:T(8,128)(2,1)S(1)}, u32[]{:S(2)}, u32[]{:S(2)}) collective-permute-start(bf16[2,192,512]{2,1,0:T(8,128)(2,1)} %bitcast.8), channel_id=1, source_target_pairs={{0,16},{16,0},{32,48},{48,32},{64,80},{80,64},{96,112},{112,96},{1... | collective-permute-start | bytes 1179656 | tf_op jit(solution)/shard_map/ppermute | solution.py:448
  142.3 0.0 copy-done.1
  142.3 0.0 copy-done.2
  142.3 1.3 combine.1
  143.5 0.3 collective-permute-done.got_ref
  143.8 0.0 copy-done
  143.8 0.9 scale.1
Async XLA Ops:
  7.2 75.0 %all-gather.3.cloned.1.call-start = ((), (), s32[]{:S(2)}) async-start(), calls=%async_computation.4 | async-start | bytes 6684672 | tf_op jit(solution)/shard_map/all_gather | solution.py:384
  11.9 127.2 %reduce-scatter.2.cloned.1.call-start = ((), (), s32[]{:S(2)}) async-start(), calls=%async_computation.3 | async-start | bytes 3538944 | tf_op jit(solution)/shard_map/reduce_scatter | solution.py:426
  99.6 42.6 %copy-start.1 = (s32[128,8]{0,1:T(8,128)S(1)}, s32[128,8]{0,1:T(8,128)}, u32[]{:S(2)}) copy-start(s32[128,8]{0,1:T(8,128)} %param.9) | copy-start | bytes 12292
  99.6 42.6 %copy-start.2 = (f32[128,8]{0,1:T(8,128)S(1)}, f32[128,8]{0,1:T(8,128)}, u32[]{:S(2)}) copy-start(f32[128,8]{0,1:T(8,128)} %param.10) | copy-start | bytes 12292
  139.1 4.7 %copy-start = (bf16[1,2,192,512]{3,2,1,0:T(8,128)(2,1)S(1)}, bf16[1,2,192,512]{3,2,1,0:T(8,128)(2,1)}, u32[]{:S(2)}) copy-start(bf16[1,2,192,512]{3,2,1,0:T(8,128)(2,1)} %reduce-scatter.2.cloned.1.call-done) | copy-start | bytes 1179652
  139.1 4.7 %collective-permute-start = (bf16[2,192,512]{2,1,0:T(8,128)(2,1)}, bf16[2,192,512]{2,1,0:T(8,128)(2,1)S(1)}, u32[]{:S(2)}, u32[]{:S(2)}) collective-permute-start(bf16[2,192,512]{2,1,0:T(8,128)(2,1)} %bitcast.8), channel_id=1, source_target_pairs={{0,16},{16,0},{32,48},{48,32},{64,80},{80,64},{96,112},{112,96},{1... | collective-permute-start | bytes 1179656 | tf_op jit(solution)/shard_map/ppermute | solution.py:448
Sparse Core Ops, SparseCore 0:
  12.0 50.2 all-gather.2
  95.2 43.8 reduce-scatter.1

commit v9 on v8

--- a/solution.py
+++ b/solution.py
@@ -109,10 +109,8 @@
     before = jnp.where(earlier < later, 1.0, 0.0).astype(BF16)
     ranks = dot(named.astype(BF16), before, 1, 0)
     keys = jnp.where(named > 0.0, ranks, -1.0)
-    for copy in packing + loads:
+    for copy in loads:
         copy.wait()
-    packed_out = pltpu.make_async_copy(packed_buf, packed_ref, weight_sems.at[len(packing)])
-    packed_out.start()
     tokens = tokens_buf[...]
     grads = jnp.concatenate([grads_buf[...], grads_buf[...]], axis=0)
     block = experts // SEND_CHUNKS
@@ -135,6 +133,11 @@
             pltpu.make_async_copy(send_buf.at[here], send_ref.at[here], send_sems.at[i])
         )
         sends[i].start()
+        if i == 0:
+            for copy in packing:
+                copy.wait()
+            packed_out = pltpu.make_async_copy(packed_buf, packed_ref, weight_sems.at[4])
+            packed_out.start()
     for copy in [packed_out] + sends:
         copy.wait()
 

time: 152 us -> 152 us (level)
  no operation moved by 1% of the time
where the time goes in v9:
time: 152 us
  blocking collectives  109 us (72%)
  Pallas kernels  24.4 us (16%)
  between operations  14.1 us (9%)
  starting transfers between devices  3.52 us (2%)
    all_to_all x2, blocking collectives, exchange(): lax.all_to_all(x, ('dp', 'expert'), split_axis=0, concat_axis=0, tiled=Tr...  109 us
    pallas_call x1, Pallas kernels, shards(): pl.pallas_call(expert_kernel, in_specs=[smem, anywhere, anywhere], out_sp...  12.9 us
    pallas_call x1, Pallas kernels, shards(): pl.pallas_call(functools.partial(dispatch_kernel, members, experts), in_s...  4.76 us
    pallas_call x1, Pallas kernels, shards(): pl.pallas_call(input_kernel, in_specs=[smem, vmem, vmem, anywhere], out_s...  4.51 us
    ppermute x1, starting transfers between devices, shards(): got = lax.ppermute(sums, 'dp', [(i, i ^ 1) for i in range(dp_size)])  3.44 us
  transfers between devices with their start and end apart: 3, of which 2 were waited for; matrix products, arithmetic and copies ran while one was open for 0% of the time, Pallas kernels for 4%

profile of v9, /device:TPU:1, one launch (start us, length us, event | category | flops | bytes accessed | tf_op | source)
XLA Modules:
  0.0 151.8 jit_solution(490576987013682593)
XLA Ops:
  7.2 0.0 all-gather.3.cloned.1.call-start
  7.2 4.8 %dispatch.1 = (bf16[1280,2048]{1,0:T(8,128)(2,1)}, bf16[1280,128]{1,0:T(8,128)(2,1)S(1)}, bf16[2,192,512]{2,1,0:T(8,128)(2,1)}) custom-call(s32[8,128]{1,0:T(8,128)} %bitcast.10, f32[8,128]{1,0:T(8,128)} %bitcast.12, bf16[128,1024]{1,0:T(8,128)(2,1)} %tokens_ref.1, bf16[128,1024]{1,0:T(8,128)(2,1)} %grads_ref.1, bf16[2,64,512]{2,1,0:T(8,128)(2,1)} %w_gate_ref.1, ...), custom_call_target="tpu_custom_call" | custom-call | tf_op jit(solution)/shard_map/dispatch/pallas_call | solution.py:366
  12.0 0.0 all-gather.3.cloned.1.call-update
  12.0 0.0 reduce-scatter.2.cloned.1.call-start
  12.1 70.2 %all_to_all.10 = bf16[32,40,2048]{2,1,0:T(8,128)(2,1)} all-to-all(bf16[32,40,2048]{2,1,0:T(8,128)(2,1)} %bitcast.17), channel_id=1, replica_groups={{0,1,2,3,4,5,6,7,8,9,10,11,12,13,14,15,16,17,18,19,20,21,22,23,24,25,26..., dimensions={0} | all-to-all | bytes 10485760 | tf_op jit(solution)/shard_map/all_to_all | solution.py:395
  82.3 0.0 all-gather.3.cloned.1.call-done
  82.3 12.9 %expert.1 = (bf16[8,2,192,512]{3,2,1,0:T(8,128)(2,1)}, bf16[1280,1024]{1,0:T(8,128)(2,1)S(1)}, bf16[32,8,256]{2,1,0:T(8,128)(2,1)S(1)}) custom-call(s32[1]{0:T(128)} %bitcast.1.core_ref, bf16[1280,2048]{1,0:T(8,128)(2,1)} %bitcast.16, bf16[16,2,192,512]{3,2,1,0:T(8,128)(2,1)} %bitcast.14), custom_call_target="tpu_custom_call" | custom-call | tf_op jit(solution)/shard_map/expert/pallas_call | solution.py:406
  95.2 0.0 reduce-scatter.2.cloned.1.call-update
  95.2 4.5 %inputs.1 = bf16[32,21,8,256]{3,2,1,0:T(8,128)(2,1)S(1)} custom-call(s32[1]{0:T(128)} %bitcast.1.core_ref, bf16[1280,1024]{1,0:T(8,128)(2,1)S(1)} %get-tuple-element.25.grads_ref, bf16[32,8,256]{2,1,0:T(8,128)(2,1)S(1)} %get-tuple-element.26.gate_ref, bf16[16,2,192,512]{3,2,1,0:T(8,128)(2,1)} %bitcast.15), custom_call_target="tpu_custom_call" | custom-call | tf_op jit(solution)/shard_map/inputs/pallas_call | solution.py:438
  99.7 0.0 copy-start.1
  99.8 0.0 copy-start.2
  99.8 39.0 %all_to_all.11.back_ref = bf16[32,21,8,256]{3,2,1,0:T(8,128)(2,1)S(1)} all-to-all(bf16[32,21,8,256]{3,2,1,0:T(8,128)(2,1)S(1)} %inputs.1), channel_id=1, replica_groups={{0,1,2,3,4,5,6,7,8,9,10,11,12,13,14,15,16,17,18,19,20,21,22,23,24,25,26..., dimensions={0} | all-to-all | bytes 5505024 | tf_op jit(solution)/shard_map/all_to_all | solution.py:395
  138.8 0.2 reduce-scatter.2.cloned.1.call-done
  139.0 0.0 copy-start
  139.0 3.4 %collective-permute-start = (bf16[2,192,512]{2,1,0:T(8,128)(2,1)}, bf16[2,192,512]{2,1,0:T(8,128)(2,1)S(1)}, u32[]{:S(2)}, u32[]{:S(2)}) collective-permute-start(bf16[2,192,512]{2,1,0:T(8,128)(2,1)} %bitcast.8), channel_id=1, source_target_pairs={{0,16},{16,0},{32,48},{48,32},{64,80},{80,64},{96,112},{112,96},{1... | collective-permute-start | bytes 1179656 | tf_op jit(solution)/shard_map/ppermute | solution.py:451
  142.4 0.0 copy-done.1
  142.4 0.0 copy-done.2
  142.4 1.3 combine.1
  143.7 0.3 collective-permute-done.got_ref
  144.0 0.0 copy-done
  144.0 0.9 scale.1
Async XLA Ops:
  7.2 75.1 %all-gather.3.cloned.1.call-start = ((), (), s32[]{:S(2)}) async-start(), calls=%async_computation.4 | async-start | bytes 6684672 | tf_op jit(solution)/shard_map/all_gather | solution.py:387
  12.0 127.0 %reduce-scatter.2.cloned.1.call-start = ((), (), s32[]{:S(2)}) async-start(), calls=%async_computation.3 | async-start | bytes 3538944 | tf_op jit(solution)/shard_map/reduce_scatter | solution.py:429
  99.7 42.7 %copy-start.1 = (s32[128,8]{0,1:T(8,128)S(1)}, s32[128,8]{0,1:T(8,128)}, u32[]{:S(2)}) copy-start(s32[128,8]{0,1:T(8,128)} %param.9) | copy-start | bytes 12292
  99.8 42.7 %copy-start.2 = (f32[128,8]{0,1:T(8,128)S(1)}, f32[128,8]{0,1:T(8,128)}, u32[]{:S(2)}) copy-start(f32[128,8]{0,1:T(8,128)} %param.10) | copy-start | bytes 12292
  139.0 5.0 %copy-start = (bf16[1,2,192,512]{3,2,1,0:T(8,128)(2,1)S(1)}, bf16[1,2,192,512]{3,2,1,0:T(8,128)(2,1)}, u32[]{:S(2)}) copy-start(bf16[1,2,192,512]{3,2,1,0:T(8,128)(2,1)} %reduce-scatter.2.cloned.1.call-done) | copy-start | bytes 1179652
  139.0 5.0 %collective-permute-start = (bf16[2,192,512]{2,1,0:T(8,128)(2,1)}, bf16[2,192,512]{2,1,0:T(8,128)(2,1)S(1)}, u32[]{:S(2)}, u32[]{:S(2)}) collective-permute-start(bf16[2,192,512]{2,1,0:T(8,128)(2,1)} %bitcast.8), channel_id=1, source_target_pairs={{0,16},{16,0},{32,48},{48,32},{64,80},{80,64},{96,112},{112,96},{1... | collective-permute-start | bytes 1179656 | tf_op jit(solution)/shard_map/ppermute | solution.py:451
Sparse Core Ops, SparseCore 0:
  12.1 50.2 all-gather.2
  95.3 43.6 reduce-scatter.1
